TPU v7x, 1024 devices: a whole 4x4x32 slice. The times are simulated.
1024 devices in a mesh: row: 8 (over x, z_hi), col: 32 (over z_lo, core), pair: 4 (over y).
Axes of the slice: x: 4, y: 4, z: 32 (z_hi: 2, z_lo: 16; z = z_hi * 16 + z_lo), core: 2. Of those that a mesh axis runs over, the one named last changes fastest.
Arguments:
- factors: bfloat16 [1800, 512, 16], P('pair', ('row', 'col')), may hold values from -1 to 1
- amplitudes: bfloat16 [40, 16, 16], P('pair'), may hold values from -0.796875 to 0.796875
- virt_irreps: int32 [512], replicated, may hold values from 0 to 3
- win_irreps: int32 [16], replicated, may hold values from 0 to 3
- occ_irreps: int32 [120], replicated, may hold values from 0 to 3
- pair_list: int32 [40, 2], replicated, may hold values from 0 to 119
Outputs:
- ladder: float32 [40, 512, 8, 64], P('pair', 'row', None, 'col')
All inputs are finite; a program needn't handle non-finite values.
Results may differ from a plain program's by a relative error of at most 0.0003.
Values may be sent and summed in bfloat16 or wider, within the bound.
A program may use at most 32 MiB of HBM per device.

v0:
```python
import jax
import jax.numpy as jnp
from jax import lax
from jax.sharding import PartitionSpec as P


def lookup_symmetry(occ_irreps, pair_list):
    labels = jnp.arange(occ_irreps.shape[0], dtype=jnp.int32)
    onehot = pair_list[:, :, None] == labels[None, None, :]
    picked = jnp.sum(jnp.where(onehot, occ_irreps[None, None, :], 0), axis=-1)
    return jnp.bitwise_xor(picked[:, 0], picked[:, 1])


def mask_amplitudes(amplitudes, win_irreps, symmetry):
    product = jnp.bitwise_xor(win_irreps[:, None], win_irreps[None, :])
    allowed = product[None, :, :] == symmetry[:, None, None]
    return jnp.where(allowed, amplitudes.astype(jnp.float32), 0.0)


def body(factors, amplitudes, virt_irreps, win_irreps, occ_irreps, pair_list):
    per_device = factors.shape[1]
    n_rows = lax.axis_size("row")
    n_cols = lax.axis_size("col")
    block_a = per_device * n_cols
    slab = amplitudes.shape[0]
    symmetry_all = lookup_symmetry(occ_irreps, pair_list)
    own_symmetry = lax.dynamic_slice_in_dim(symmetry_all, lax.axis_index("pair") * slab, slab)
    operand = lax.all_gather(factors, "pair", axis=0, tiled=True)
    weights = mask_amplitudes(amplitudes, win_irreps, own_symmetry)
    n_fitting = operand.shape[0]
    width = operand.shape[2]
    b_rows = lax.all_gather(operand, "row", axis=1, tiled=True)
    b_matrix = b_rows.reshape(n_fitting, n_rows * per_device * width)
    panel_rows = lax.all_gather(operand, "col", axis=1, tiled=True)
    count = panel_rows.shape[1]
    integral = lax.dot_general(
        panel_rows.reshape(n_fitting, count * width),
        b_matrix,
        (((0,), (0,)), ((), ())),
        preferred_element_type=jnp.float32,
    )
    integral = integral.reshape(count, width, n_rows * per_device, width)
    result = jnp.einsum("acbd,pcd->pab", integral, weights, precision=lax.Precision.HIGHEST)
    partial_sum = result.reshape(weights.shape[0], count, n_rows, per_device)
    a_labels = lax.dynamic_slice_in_dim(virt_irreps, lax.axis_index("row") * block_a, block_a)
    b_labels = lax.dynamic_slice_in_dim(
        virt_irreps.reshape(n_rows, -1), lax.axis_index("col") * per_device, per_device, 1
    )
    pair_sym = jnp.bitwise_xor(a_labels[:, None, None], b_labels[None, :, :])
    allowed = pair_sym[None, :, :, :] == own_symmetry[:, None, None, None]
    return jnp.where(allowed, partial_sum, 0.0)


def solution(mesh):
    in_specs = (P("pair", ("row", "col"), None), P("pair", None, None), P(), P(), P(), P())
    out_specs = P("pair", "row", None, "col")
    return jax.shard_map(body, mesh=mesh, in_specs=in_specs, out_specs=out_specs, check_vma=False)
```

profile of v0, /device:TPU:4, one launch (start us, length us, event | category | flops | bytes accessed | tf_op | source)
XLA Modules:
  0.0 428.1 jit_solution(9962040087748574257)
XLA Ops:
  6.5 0.0 all-gather.2.cloned.1.call-start
  6.5 0.9 copy.21
  7.5 14.3 %all_gather.9 = bf16[1800,2,16]{2,1,0:T(2,128)(2,1)S(1)} all-gather(bf16[450,2,16]{2,1,0:T(2,128)(2,1)S(1)} %copy.21), channel_id=1, replica_groups=mesh['row'=8,'col'=32,'pair'=4] {'pair'}, dimensions={0}, use_global_device_ids=true | all-gather | bytes 144000 | tf_op jit(solution)/shard_map/all_gather | solution.py:28
  21.7 1.8 copy.22
  23.6 0.0 all-gather.2.cloned.1.call-update
  23.6 0.8 reshape.51
  24.3 0.8 dynamic_slice.11
  25.1 0.9 select_reduce_fusion
  26.0 0.1 dynamic-slice_bitcast_fusion
  26.1 0.1 constant_dynamic-slice_fusion
  26.1 0.8 broadcast_xor_fusion
  26.9 0.1 broadcast_xor_fusion.1
  27.0 0.9 convert_select_fusion
  27.9 187.5 %all_gather.11 = bf16[1800,16,16]{0,2,1:T(8,128)(2,1)S(1)} all-gather(bf16[1800,2,16]{0,2,1:T(8,128)(2,1)} %copy.22), channel_id=1, replica_groups=mesh['row'=8,'col'=32,'pair'=4] {'row'}, dimensions={1}, use_global_device_ids=true | all-gather | bytes 1036800 | tf_op jit(solution)/shard_map/all_gather | solution.py:32
  215.4 198.4 %all-gather.2.cloned.1.call-done = bf16[1800,64,16]{0,2,1:T(8,128)(2,1)} async-done(((bf16[1800,2,16]{0,2,1:T(8,128)(2,1)}), bf16[1800,64,16]{0,2,1:T(8,128)(2,1)}) %all-gather.2.cloned.1.call-update) | async-done | bytes 3686416 | tf_op jit(solution)/shard_map/all_gather | solution.py:34
  413.8 4.5 %fusion = f32[64,16,16,16]{0,3,1,2:T(8,128)S(1)} fusion(bf16[64,16,1800]{2,1,0:T(8,128)(2,1)} %bitcast.30, bf16[1800,16,16]{0,2,1:T(8,128)(2,1)S(1)} %all_gather.11), kind=kOutput, calls=%fused_computation | convolution fusion | flops 943718400 | bytes 5656576 | tf_op jit(solution)/shard_map/dot_general | solution.py:36
  418.2 2.3 fusion.4
  420.5 0.7 compare_select_fusion
  (1 shorter events, 0.0 us)
Async XLA Ops:
  6.5 407.2 %all-gather.2.cloned.1.call-start = ((), (), s32[]{:S(2)}) async-start(), calls=%async_computation | async-start | bytes 4055040 | tf_op jit(solution)/shard_map/all_gather | solution.py:34
Sparse Core Ops, SparseCore 0:
  23.7 390.0 all-gather.1
where the time goes:
time: 429 us; the launch traced here: 428 us
  blocking collectives  202 us (47%)
  waiting for transfers between devices  198 us (46%)
  between operations  13.4 us (3%)
  matrix products  6.78 us (2%)
  local copies, waits for them, and re-layouts  4.41 us (1%)
    all_gather x1, waiting for transfers between devices, body(): panel_rows = lax.all_gather(operand, 'col', axis=1, tiled=True)  198 us
    all_gather x1, blocking collectives, body(): b_rows = lax.all_gather(operand, 'row', axis=1, tiled=True)  187 us
    all_gather x1, blocking collectives, body(): operand = lax.all_gather(factors, 'pair', axis=0, tiled=True)  14.3 us
  transfers between devices with their start and end apart: 1, of which 1 were waited for; matrix products, arithmetic and copies ran while one was open for 1% of the time, Pallas kernels for 0%

commit v1 on v0

--- a/solution.py
+++ b/solution.py
@@ -25,13 +25,13 @@
     slab = amplitudes.shape[0]
     symmetry_all = lookup_symmetry(occ_irreps, pair_list)
     own_symmetry = lax.dynamic_slice_in_dim(symmetry_all, lax.axis_index("pair") * slab, slab)
-    operand = lax.all_gather(factors, "pair", axis=0, tiled=True)
-    weights = mask_amplitudes(amplitudes, win_irreps, own_symmetry)
-    n_fitting = operand.shape[0]
-    width = operand.shape[2]
-    b_rows = lax.all_gather(operand, "row", axis=1, tiled=True)
+    all_amplitudes = lax.all_gather(amplitudes, "pair", axis=0, tiled=True)
+    weights = mask_amplitudes(all_amplitudes, win_irreps, symmetry_all)
+    n_fitting = factors.shape[0]
+    width = factors.shape[2]
+    b_rows = lax.all_gather(factors, "row", axis=1, tiled=True)
     b_matrix = b_rows.reshape(n_fitting, n_rows * per_device * width)
-    panel_rows = lax.all_gather(operand, "col", axis=1, tiled=True)
+    panel_rows = lax.all_gather(factors, "col", axis=1, tiled=True)
     count = panel_rows.shape[1]
     integral = lax.dot_general(
         panel_rows.reshape(n_fitting, count * width),
@@ -40,15 +40,16 @@
         preferred_element_type=jnp.float32,
     )
     integral = integral.reshape(count, width, n_rows * per_device, width)
-    result = jnp.einsum("acbd,pcd->pab", integral, weights, precision=lax.Precision.HIGHEST)
-    partial_sum = result.reshape(weights.shape[0], count, n_rows, per_device)
+    partial = jnp.einsum("acbd,pcd->pab", integral, weights, precision=lax.Precision.HIGHEST)
+    total = lax.psum_scatter(partial, "pair", scatter_dimension=0, tiled=True)
+    total = total.reshape(slab, count, n_rows, per_device)
     a_labels = lax.dynamic_slice_in_dim(virt_irreps, lax.axis_index("row") * block_a, block_a)
     b_labels = lax.dynamic_slice_in_dim(
         virt_irreps.reshape(n_rows, -1), lax.axis_index("col") * per_device, per_device, 1
     )
     pair_sym = jnp.bitwise_xor(a_labels[:, None, None], b_labels[None, :, :])
     allowed = pair_sym[None, :, :, :] == own_symmetry[:, None, None, None]
-    return jnp.where(allowed, partial_sum, 0.0)
+    return jnp.where(allowed, total, 0.0)
 
 
 def solution(mesh):

time: 429 us -> 282 us (0.66)
  the two profiles are of different devices: /device:TPU:4 before, /device:TPU:1 now
where the time goes in v1:
time: 282 us; the launch traced here: 280 us
  blocking collectives  228 us (81%)
  waiting for transfers between devices  31.3 us (11%)
  between operations  13.5 us (5%)
  other arithmetic  3.49 us (1%)
  matrix products  2.86 us (1%)
    all_gather x1, blocking collectives, body(): panel_rows = lax.all_gather(factors, 'col', axis=1, tiled=True)  119 us
    all_gather x1, blocking collectives, body(): b_rows = lax.all_gather(factors, 'row', axis=1, tiled=True)  96 us
    reduce_scatter x1, waiting for transfers between devices, body(): total = lax.psum_scatter(partial, 'pair', scatter_dimension=0, tiled=True)  31.3 us
    all_gather x1, blocking collectives, body(): all_amplitudes = lax.all_gather(amplitudes, 'pair', axis=0, tiled=True)  13.2 us
  transfers between devices with their start and end apart: 1, of which 1 were waited for; matrix products, arithmetic and copies ran while one was open for 0% of the time, Pallas kernels for 0%

profile of v1, /device:TPU:1, one launch (start us, length us, event | category | flops | bytes accessed | tf_op | source)
XLA Modules:
  0.0 280.1 jit_solution(11314217571865350983)
XLA Ops:
  6.5 0.0 reduce-scatter.2.cloned.1.call-start
  6.5 118.5 %all_gather.10 = bf16[450,64,16]{0,2,1:T(8,128)(2,1)S(1)} all-gather(bf16[450,2,16]{0,2,1:T(8,128)(2,1)} %param.6), channel_id=1, replica_groups=mesh['row'=8,'col'=32,'pair'=4] {'col'}, dimensions={1}, use_global_device_ids=true | all-gather | bytes 950400 | tf_op jit(solution)/shard_map/all_gather | solution.py:34
  125.1 96.0 %all_gather.11 = bf16[450,16,16]{0,2,1:T(8,128)(2,1)S(1)} all-gather(bf16[450,2,16]{0,2,1:T(8,128)(2,1)} %param.6), channel_id=1, replica_groups=mesh['row'=8,'col'=32,'pair'=4] {'row'}, dimensions={1}, use_global_device_ids=true | all-gather | bytes 259200 | tf_op jit(solution)/shard_map/all_gather | solution.py:32
  221.1 13.2 %all_gather.9 = bf16[40,16,16]{2,1,0:T(8,128)(2,1)S(1)} all-gather(bf16[10,16,16]{2,1,0:T(8,128)(2,1)} %param.7), channel_id=1, replica_groups=mesh['row'=8,'col'=32,'pair'=4] {'pair'}, dimensions={0}, use_global_device_ids=true | all-gather | bytes 25600 | tf_op jit(solution)/shard_map/all_gather | solution.py:28
  234.2 0.8 broadcast_xor_fusion
  235.0 0.9 select_reduce_fusion
  235.9 0.1 convert_select_fusion
  236.0 0.2 copy.16
  236.2 1.5 fusion
  237.7 0.0 copy-start
  237.8 1.3 convolution_bitcast_fusion
  239.1 0.8 copy.17
  239.9 0.0 reduce-scatter.2.cloned.1.call-update
  239.9 0.0 copy-done
  239.9 0.1 reshape.59
  240.0 0.1 dynamic_slice.11
  240.1 0.1 constant_dynamic-slice_fusion
  240.1 0.1 dynamic-slice_bitcast_fusion
  240.2 0.1 broadcast_xor_fusion.1
  240.3 31.3 %reduce-scatter.2.cloned.1.call-done = f32[10,64,16]{1,2,0:T(8,128)} async-done(((f32[40,64,16]{1,2,0:T(8,128)}), f32[10,64,16]{1,2,0:T(8,128)}) %reduce-scatter.2.cloned.1.call-update) | async-done | bytes 40976 | tf_op jit(solution)/shard_map/reduce_scatter | solution.py:44
  271.6 1.6 compare_select_fusion
  (2 shorter events, 0.0 us)
Async XLA Ops:
  6.5 265.1 %reduce-scatter.2.cloned.1.call-start = ((), (), s32[]{:S(2)}) async-start(), calls=%async_computation.1 | async-start | bytes 409600 | tf_op jit(solution)/shard_map/reduce_scatter | solution.py:44
  237.7 2.2 copy-start
Sparse Core Ops, SparseCore 0:
  240.0 31.5 reduce-scatter.1

commit v2 on v0

v2 whole, which is shorter than its diff:
```python
import functools

import jax
import jax.numpy as jnp
from jax import lax
from jax.experimental import pallas as pl
from jax.experimental.pallas import tpu as pltpu
from jax.sharding import PartitionSpec as P

MESH = pl.DeviceIdType.MESH
LANES = 512
GROUP = 4


def kernel(
    dims, x_ref, amp_ref, virt_ref, win_ref, occ_ref, pairs_ref, out_ref,
    a_buf, b_buf, w_buf, wide, integral, parts, sums, inbox,
    a_send, a_recv, b_send, b_recv, w_send, w_recv, r_send, r_recv,
):
    n_rows, n_cols, n_pairs, slab = dims
    row, col, pair = lax.axis_index("row"), lax.axis_index("col"), lax.axis_index("pair")
    width = amp_ref.shape[2]
    height = 2 * width
    n_fit = x_ref.shape[2]
    n_groups = n_cols // 2 // GROUP
    n_x = n_rows // 2
    core = lax.rem(col, 2)
    place = lax.rem(lax.div(col, 2), GROUP)
    group = lax.div(lax.div(col, 2), GROUP)

    def column(g, p):
        return (g * GROUP + p) * 2 + core

    def at(r=None, c=None, p=None):
        return (row if r is None else r, col if c is None else c, pair if p is None else p)

    far = [column(jnp.bitwise_xor(group, k), place) for k in range(1, n_groups)]
    near = [column(group, jnp.bitwise_xor(place, j)) for j in range(1, GROUP)]
    mate = jnp.bitwise_xor(col, 1)
    partner = jnp.bitwise_xor(row, 1)
    sides = [jnp.bitwise_xor(row, 2 * k) for k in range(1, n_x)]
    others = [jnp.bitwise_xor(pair, k) for k in range(1, n_pairs)]

    peers = [at(c=c) for c in far + near + [mate]]
    peers += [at(r=r) for r in [partner] + sides] + [at(p=p) for p in others]
    barrier = pltpu.get_barrier_semaphore()
    for peer in peers:
        pl.semaphore_signal(barrier, inc=1, device_id=peer, device_id_type=MESH)

    own = jnp.concatenate([x_ref[0], x_ref[1]], axis=0)
    own = jnp.concatenate([own, jnp.zeros((height, LANES - n_fit), own.dtype)], axis=1)
    a_buf[col] = own
    b_buf[row] = own

    symmetry = []
    for s in range(slab):
        first, second = pairs_ref[0, pair * slab + s], pairs_ref[1, pair * slab + s]
        symmetry.append(jnp.bitwise_xor(occ_ref[first], occ_ref[second]))
    down = lax.broadcasted_iota(jnp.int32, (width, width), 0)
    across = lax.broadcasted_iota(jnp.int32, (width, width), 1)
    product = jnp.zeros((width, width), jnp.int32)
    for j in range(width):
        label = win_ref[j]
        product = jnp.bitwise_xor(product, jnp.where(down == j, label, 0))
        product = jnp.bitwise_xor(product, jnp.where(across == j, label, 0))
    for s in range(slab):
        kept = jnp.where(product == symmetry[s], amp_ref[s].astype(jnp.float32), 0.0)
        w_buf[pair, s * width:(s + 1) * width, :] = kept.astype(jnp.bfloat16)

    pl.semaphore_wait(barrier, len(peers))
    started = []

    def send(src, dst, sems, slot, recv, target):
        copy = pltpu.make_async_remote_copy(
            src_ref=src, dst_ref=dst, send_sem=sems.at[slot], recv_sem=recv, device_id=target, device_id_type=MESH
        )
        copy.start()
        started.append(copy)

    counts = {"a": 0, "b": 0}

    def send_a(slot, c):
        send(a_buf.at[slot], a_buf.at[slot], a_send, counts["a"], a_recv.at[slot], at(c=c))
        counts["a"] += 1

    def send_b(slot, r):
        send(b_buf.at[slot], b_buf.at[slot], b_send, counts["b"], b_recv.at[slot], at(r=r))
        counts["b"] += 1

    def arrived(buf, recv, sems, slot, peer):
        pltpu.make_async_remote_copy(
            src_ref=buf.at[slot], dst_ref=buf.at[slot], send_sem=sems.at[0], recv_sem=recv.at[slot],
            device_id=peer, device_id_type=MESH,
        ).wait_recv()

    send_b(row, partner)
    for c in reversed(far):
        send_a(col, c)
    for c in near:
        send_a(col, c)
    for i, p in enumerate(others):
        send(w_buf.at[pair], w_buf.at[pair], w_send, i, w_recv.at[pair], at(p=p))
    for r in sides:
        send_b(row, r)
    send_a(col, mate)

    def relay(slot, source):
        arrived(a_buf, a_recv, a_send, slot, at(c=source))
        for c in near:
            send_a(slot, c)
        send_a(slot, mate)

    def handover(slot, source):
        arrived(a_buf, a_recv, a_send, slot, at(c=source))
        send_a(slot, mate)

    span = n_rows * 2 * width
    spread = (
        lax.rem(lax.broadcasted_iota(jnp.int32, (width, span), 1), width)
        == lax.broadcasted_iota(jnp.int32, (width, span), 0)
    ).astype(jnp.bfloat16)
    own_b = (
        lax.div(lax.broadcasted_iota(jnp.int32, (n_rows * 2, span), 1), width)
        == lax.broadcasted_iota(jnp.int32, (n_rows * 2, span), 0)
    )

    def expand(p):
        def one(s, carry):
            lines = jnp.dot(
                w_buf[p, pl.ds(pl.multiple_of(s * width, width), width), :], spread, preferred_element_type=jnp.float32
            )
            start = pl.multiple_of((p * slab + s) * n_rows * 2, n_rows * 2)
            for c in range(width):
                block = jnp.where(own_b, jnp.broadcast_to(lines[c:c + 1, :], own_b.shape), 0.0)
                wide[pl.ds(start, n_rows * 2), c * span:(c + 1) * span] = block.astype(jnp.bfloat16)
            return carry

        lax.fori_loop(0, slab, one, 0)

    expand(pair)
    relay(far[0], far[0])
    for j, c in enumerate(near):
        handover(c, c)
    for p in others[:1]:
        arrived(w_buf, w_recv, w_send, p, at(p=p))
        expand(p)
    relay(far[1], far[1])
    for p in others[1:]:
        arrived(w_buf, w_recv, w_send, p, at(p=p))
        expand(p)
    relay(far[2], far[2])
    for j in range(1, GROUP):
        slot = column(jnp.bitwise_xor(group, 1), jnp.bitwise_xor(place, j))
        handover(slot, near[j - 1])
    arrived(b_buf, b_recv, b_send, partner, at(r=partner))
    for r in sides:
        send_b(partner, r)
    for k in range(2, n_groups):
        for j in range(1, GROUP):
            slot = column(jnp.bitwise_xor(group, k), jnp.bitwise_xor(place, j))
            handover(slot, near[j - 1])
    for r in sides:
        arrived(b_buf, b_recv, b_send, r, at(r=r))
        arrived(b_buf, b_recv, b_send, jnp.bitwise_xor(r, 1), at(r=r))
    for c in range(n_cols // 2):
        slot = 2 * c + 1 - core
        arrived(a_buf, a_recv, a_send, slot, at(c=mate))

    n_a = 2 * n_cols
    b_all = b_buf[...].reshape(span, LANES)
    chunk = 8

    def multiply(i, carry):
        first = pl.multiple_of(i * chunk, chunk)
        rows = a_buf[pl.ds(first, chunk)].reshape(chunk * height, LANES)
        tile = lax.dot_general(rows, b_all, (((1,), (1,)), ((), ())), preferred_element_type=jnp.float32)
        for t in range(span // 128):
            integral[t, pl.ds(pl.multiple_of(first * height, chunk * height), chunk * height), :] = (
                tile[:, t * 128:(t + 1) * 128]
            )
        return carry

    lax.fori_loop(0, n_cols // chunk, multiply, 0)
    for c in range(width):
        for t in range(span // 128):
            lines = integral[t, pl.ds(c, n_a, stride=width), :]
            high = lines.astype(jnp.bfloat16)
            first = c * span + t * 128
            parts[0:n_a, first:first + 128] = high
            parts[n_a:2 * n_a, first:first + 128] = (lines - high.astype(jnp.float32)).astype(jnp.bfloat16)

    tall = slab * n_rows * 2
    half = tall // 2

    def residual(p):
        start = pl.multiple_of(p * tall, tall)
        both = lax.dot_general(
            wide[pl.ds(start, tall), :], parts[...], (((1,), (1,)), ((), ())), preferred_element_type=jnp.float32
        )
        whole = both[:, 0:n_a] + both[:, n_a:2 * n_a]
        return jnp.concatenate([whole[0:half], whole[half:tall]], axis=1)

    for i, p in enumerate(others):
        sums[p] = residual(p)
        send(sums.at[p], inbox.at[pair], r_send, i, r_recv.at[pair], at(p=p))
    total = residual(pair)

    lane = lax.broadcasted_iota(jnp.int32, (n_rows * 2, 2 * n_a), 1)
    line = lax.broadcasted_iota(jnp.int32, (n_rows * 2, 2 * n_a), 0)
    label = jnp.zeros((n_rows * 2, 2 * n_a), jnp.int32)
    lane_a = lax.rem(lane, n_a)
    for j in range(n_a):
        label = jnp.where(lane_a == j, virt_ref[row * n_a + j], label)
    for k in range(n_rows):
        for m in range(2):
            label = jnp.bitwise_xor(label, jnp.where(line == 2 * k + m, virt_ref[k * n_a + col * 2 + m], 0))

    for p in others:
        arrived(inbox, r_recv, r_send, p, at(p=p))
        total = total + inbox[p]
    deep = n_rows * 2
    for s in range(slab // 2):
        wanted = jnp.where(lane < n_a, symmetry[s], symmetry[s + slab // 2])
        kept = jnp.where(label == wanted, total[s * deep:(s + 1) * deep], 0.0)
        out_ref[s] = kept[:, 0:n_a]
        out_ref[s + slab // 2] = kept[:, n_a:2 * n_a]
    for copy in started:
        copy.wait_send()


def body(factors, amplitudes, virt_irreps, win_irreps, occ_irreps, pair_list):
    n_rows, n_cols, n_pairs = (lax.axis_size(name) for name in ("row", "col", "pair"))
    slab, width = amplitudes.shape[0], amplitudes.shape[1]
    per_device = factors.shape[1]
    n_a = per_device * n_cols
    span = n_rows * per_device * width
    n_b = n_rows * per_device
    n_groups = n_cols // 2 // GROUP
    n_x = n_rows // 2
    height = per_device * width
    a_sends = (n_groups - 1) + n_groups * (GROUP - 1) + n_cols // 2
    b_sends = 1 + 2 * (n_x - 1)
    vmem, smem = pl.BlockSpec(memory_space=pltpu.VMEM), pl.BlockSpec(memory_space=pltpu.SMEM)
    dma = pltpu.SemaphoreType.DMA
    out = pl.pallas_call(
        functools.partial(kernel, (n_rows, n_cols, n_pairs, slab)),
        out_shape=jax.ShapeDtypeStruct((slab, n_b, n_a), jnp.float32),
        in_specs=[vmem, vmem, smem, smem, smem, smem],
        out_specs=vmem,
        scratch_shapes=[
            pltpu.VMEM((n_cols, height, LANES), jnp.bfloat16),
            pltpu.VMEM((n_rows, height, LANES), jnp.bfloat16),
            pltpu.VMEM((n_pairs, slab * width, width), jnp.bfloat16),
            pltpu.VMEM((n_pairs * slab * n_b, width * span), jnp.bfloat16),
            pltpu.VMEM((span // 128, n_a * width, 128), jnp.float32),
            pltpu.VMEM((2 * n_a, width * span), jnp.bfloat16),
            pltpu.VMEM((n_pairs, slab * n_b // 2, 2 * n_a), jnp.float32),
            pltpu.VMEM((n_pairs, slab * n_b // 2, 2 * n_a), jnp.float32),
            dma((a_sends,)), dma((n_cols,)),
            dma((b_sends,)), dma((n_rows,)),
            dma((n_pairs,)), dma((n_pairs,)),
            dma((n_pairs,)), dma((n_pairs,)),
        ],
        compiler_params=pltpu.CompilerParams(
            collective_id=0, has_side_effects=True, vmem_limit_bytes=32 * 1024 * 1024
        ),
        name="ladder",
    )(jnp.transpose(factors, (1, 2, 0)), amplitudes, virt_irreps, win_irreps, occ_irreps, pair_list.T)
    return jnp.transpose(out.reshape(slab, n_rows, per_device, n_a), (0, 3, 1, 2))


def solution(mesh):
    in_specs = (P("pair", ("row", "col"), None), P("pair", None, None), P(), P(), P(), P())
    out_specs = P("pair", "row", None, "col")
    return jax.shard_map(body, mesh=mesh, in_specs=in_specs, out_specs=out_specs, check_vma=False)
```

time: 429 us -> 71.6 us (0.17)
  the two profiles are of different devices: /device:TPU:4 before, /device:TPU:1 now
where the time goes in v2:
time: 71.6 us; the launch traced here: 71.3 us
  Pallas kernels  67.7 us (95%)
  local copies, waits for them, and re-layouts  3.52 us (5%)
    pallas_call x1, Pallas kernels, body(): pl.pallas_call(functools.partial(kernel, (n_rows, n_cols, n_pairs, slab))...  67.7 us
    unnamed x13, local copies, waits for them, and re-layouts  3.52 us

profile of v2, /device:TPU:1, one launch (start us, length us, event | category | flops | bytes accessed | tf_op | source)
XLA Modules:
  0.0 71.3 jit_solution(1198788678405426449)
XLA Ops:
  0.0 0.0 copy-start.2
  0.0 0.0 copy-start.3
  0.0 0.0 copy-start.4
  0.0 0.7 copy-done.2
  0.7 0.0 copy-done.3
  0.7 0.0 copy-done.4
  0.7 0.0 copy-start
  0.7 0.8 %copy-done = bf16[10,16,16]{2,1,0:T(8,128)(2,1)S(1)} copy-done((bf16[10,16,16]{2,1,0:T(8,128)(2,1)S(1)}, bf16[10,16,16]{2,1,0:T(8,128)(2,1)}, u32[]{:S(2)}) %copy-start) | copy-done | bytes 5144
  1.5 0.0 copy-start.1
  1.5 0.8 %copy-done.1 = bf16[450,2,16]{0,2,1:T(8,128)(2,1)S(1)} copy-done((bf16[450,2,16]{0,2,1:T(8,128)(2,1)S(1)}, bf16[450,2,16]{0,2,1:T(8,128)(2,1)}, u32[]{:S(2)}) %copy-start.1) | copy-done | bytes 28824
  2.2 0.0 copy-start.5
  2.2 0.7 copy-done.5
  2.9 67.7 %ladder.1 = f32[10,16,64]{2,1,0:T(8,128)S(1)} custom-call(bf16[2,16,450]{2,1,0:T(8,128)(2,1)S(1)} %bitcast.6, bf16[10,16,16]{2,1,0:T(8,128)(2,1)S(1)} %copy-done, s32[512]{0:T(512)S(1)} %copy-done.2, s32[16]{0:T(128)S(1)} %copy-done.4, s32[120]{0:T(128)S(1)} %copy-done.5, s32[2,40]{1,0:T(2,128)S(1)} %bitcast.7), custom_call_target="tpu_custom_call" | custom-call | tf_op jit(solution)/shard_map/ladder/pallas_call | solution.py:245
  70.6 0.6 copy.8
Async XLA Ops:
  0.0 0.7 copy-start.2
  0.0 0.7 copy-start.3
  0.0 0.7 copy-start.4
  0.7 0.8 %copy-start = (bf16[10,16,16]{2,1,0:T(8,128)(2,1)S(1)}, bf16[10,16,16]{2,1,0:T(8,128)(2,1)}, u32[]{:S(2)}) copy-start(bf16[10,16,16]{2,1,0:T(8,128)(2,1)} %amp_ref.1) | copy-start | bytes 15364
  1.5 0.8 %copy-start.1 = (bf16[450,2,16]{0,2,1:T(8,128)(2,1)S(1)}, bf16[450,2,16]{0,2,1:T(8,128)(2,1)}, u32[]{:S(2)}) copy-start(bf16[450,2,16]{0,2,1:T(8,128)(2,1)} %param.6) | copy-start | bytes 86404
  2.2 0.7 copy-start.5

commit v3 on v2

--- a/solution.py
+++ b/solution.py
@@ -13,9 +13,10 @@
 
 
 def kernel(
-    dims, x_ref, amp_ref, virt_ref, win_ref, occ_ref, pairs_ref, out_ref,
+    dims, x_hbm, amp_hbm, virt_hbm, win_hbm, occ_hbm, pairs_hbm, out_ref,
+    x_ref, amp_ref, virt_ref, win_ref, occ_ref, pairs_ref, local,
     a_buf, b_buf, w_buf, wide, integral, parts, sums, inbox,
-    a_send, a_recv, b_send, b_recv, w_send, w_recv, r_send, r_recv,
+    a_send, a_recv, b_send, b_recv, w_send, w_recv, r_send, r_recv, f_send,
 ):
     n_rows, n_cols, n_pairs, slab = dims
     row, col, pair = lax.axis_index("row"), lax.axis_index("col"), lax.axis_index("pair")
@@ -41,17 +42,82 @@
     sides = [jnp.bitwise_xor(row, 2 * k) for k in range(1, n_x)]
     others = [jnp.bitwise_xor(pair, k) for k in range(1, n_pairs)]
 
-    peers = [at(c=c) for c in far + near + [mate]]
-    peers += [at(r=r) for r in [partner] + sides] + [at(p=p) for p in others]
+    higher = [jnp.bitwise_xor(group, k) > group for k in range(1, n_groups)]
+    upper = jnp.bitwise_and(row, 1) == 1
+
     barrier = pltpu.get_barrier_semaphore()
+
+    def greet(peer):
+        pl.semaphore_signal(barrier, inc=1, device_id=peer, device_id_type=MESH)
+
+    peers = [at(c=c) for c in near + [mate]] + [at(r=r) for r in sides] + [at(p=p) for p in others]
     for peer in peers:
-        pl.semaphore_signal(barrier, inc=1, device_id=peer, device_id_type=MESH)
-
+        greet(peer)
+    for c, up in zip(far, higher):
+        pl.when(up)(functools.partial(greet, at(c=c)))
+    pl.when(jnp.logical_not(upper))(functools.partial(greet, at(r=partner)))
+
+    loads = []
+    pairs_of = ((x_hbm, x_ref), (amp_hbm, amp_ref), (win_hbm, win_ref), (occ_hbm, occ_ref), (pairs_hbm, pairs_ref), (virt_hbm, virt_ref))
+    for i, (src, dst) in enumerate(pairs_of):
+        loads.append(pltpu.make_async_copy(src, dst, local.at[i]))
+        loads[i].start()
+
+    loads[0].wait()
     own = jnp.concatenate([x_ref[0], x_ref[1]], axis=0)
     own = jnp.concatenate([own, jnp.zeros((height, LANES - n_fit), own.dtype)], axis=1)
     a_buf[col] = own
     b_buf[row] = own
 
+    pl.semaphore_wait(barrier, len(peers) + group + jnp.bitwise_and(row, 1))
+    started = []
+
+    def send(src, dst, sems, slot, recv, target):
+        copy = pltpu.make_async_remote_copy(
+            src_ref=src, dst_ref=dst, send_sem=sems.at[slot], recv_sem=recv, device_id=target, device_id_type=MESH
+        )
+        copy.start()
+        started.append(copy)
+
+    counts = {"a": 0, "b": 0}
+
+    def send_a(slot, c):
+        send(a_buf.at[slot], a_buf.at[slot], a_send, counts["a"], a_recv.at[slot], at(c=c))
+        counts["a"] += 1
+
+    def send_b(slot, r):
+        send(b_buf.at[slot], b_buf.at[slot], b_send, counts["b"], b_recv.at[slot], at(r=r))
+        counts["b"] += 1
+
+    def arrived(buf, recv, sems, slot, peer):
+        pltpu.make_async_remote_copy(
+            src_ref=buf.at[slot], dst_ref=buf.at[slot], send_sem=sems.at[0], recv_sem=recv.at[slot],
+            device_id=peer, device_id_type=MESH,
+        ).wait_recv()
+
+    def to_partner():
+        pltpu.make_async_remote_copy(
+            src_ref=b_buf.at[row], dst_ref=b_buf.at[row], send_sem=b_send.at[2 * len(sides)], recv_sem=b_recv.at[row],
+            device_id=at(r=partner), device_id_type=MESH,
+        ).start()
+
+    def to_far(k):
+        pltpu.make_async_remote_copy(
+            src_ref=a_buf.at[col], dst_ref=a_buf.at[col], send_sem=f_send.at[k], recv_sem=a_recv.at[col],
+            device_id=at(c=far[k]), device_id_type=MESH,
+        ).start()
+
+    pl.when(upper)(to_partner)
+    for k in reversed(range(len(far))):
+        pl.when(jnp.logical_not(higher[k]))(functools.partial(to_far, k))
+    for c in near:
+        send_a(col, c)
+    for r in sides:
+        send_b(row, r)
+    send_a(col, mate)
+
+    for load in loads[1:]:
+        load.wait()
     symmetry = []
     for s in range(slab):
         first, second = pairs_ref[0, pair * slab + s], pairs_ref[1, pair * slab + s]
@@ -66,46 +132,13 @@
     for s in range(slab):
         kept = jnp.where(product == symmetry[s], amp_ref[s].astype(jnp.float32), 0.0)
         w_buf[pair, s * width:(s + 1) * width, :] = kept.astype(jnp.bfloat16)
-
-    pl.semaphore_wait(barrier, len(peers))
-    started = []
-
-    def send(src, dst, sems, slot, recv, target):
-        copy = pltpu.make_async_remote_copy(
-            src_ref=src, dst_ref=dst, send_sem=sems.at[slot], recv_sem=recv, device_id=target, device_id_type=MESH
-        )
-        copy.start()
-        started.append(copy)
-
-    counts = {"a": 0, "b": 0}
-
-    def send_a(slot, c):
-        send(a_buf.at[slot], a_buf.at[slot], a_send, counts["a"], a_recv.at[slot], at(c=c))
-        counts["a"] += 1
-
-    def send_b(slot, r):
-        send(b_buf.at[slot], b_buf.at[slot], b_send, counts["b"], b_recv.at[slot], at(r=r))
-        counts["b"] += 1
-
-    def arrived(buf, recv, sems, slot, peer):
-        pltpu.make_async_remote_copy(
-            src_ref=buf.at[slot], dst_ref=buf.at[slot], send_sem=sems.at[0], recv_sem=recv.at[slot],
-            device_id=peer, device_id_type=MESH,
-        ).wait_recv()
-
-    send_b(row, partner)
-    for c in reversed(far):
-        send_a(col, c)
-    for c in near:
-        send_a(col, c)
     for i, p in enumerate(others):
         send(w_buf.at[pair], w_buf.at[pair], w_send, i, w_recv.at[pair], at(p=p))
-    for r in sides:
-        send_b(row, r)
-    send_a(col, mate)
-
-    def relay(slot, source):
-        arrived(a_buf, a_recv, a_send, slot, at(c=source))
+
+    def relay(k):
+        slot = far[k]
+        arrived(a_buf, a_recv, a_send, slot, at(c=slot))
+        pl.when(higher[k])(functools.partial(to_far, k))
         for c in near:
             send_a(slot, c)
         send_a(slot, mate)
@@ -138,27 +171,35 @@
         lax.fori_loop(0, slab, one, 0)
 
     expand(pair)
-    relay(far[0], far[0])
+    relay(0)
     for j, c in enumerate(near):
         handover(c, c)
     for p in others[:1]:
         arrived(w_buf, w_recv, w_send, p, at(p=p))
         expand(p)
-    relay(far[1], far[1])
+    relay(1)
     for p in others[1:]:
         arrived(w_buf, w_recv, w_send, p, at(p=p))
         expand(p)
-    relay(far[2], far[2])
+    relay(2)
     for j in range(1, GROUP):
         slot = column(jnp.bitwise_xor(group, 1), jnp.bitwise_xor(place, j))
         handover(slot, near[j - 1])
-    arrived(b_buf, b_recv, b_send, partner, at(r=partner))
-    for r in sides:
-        send_b(partner, r)
+    def across_z():
+        arrived(b_buf, b_recv, b_send, partner, at(r=partner))
+        pl.when(jnp.logical_not(upper))(to_partner)
+        for i, r in enumerate(sides):
+            pltpu.make_async_remote_copy(
+                src_ref=b_buf.at[partner], dst_ref=b_buf.at[partner], send_sem=b_send.at[len(sides) + i],
+                recv_sem=b_recv.at[partner], device_id=at(r=r), device_id_type=MESH,
+            ).start()
+
+    pl.when(jnp.logical_not(upper))(across_z)
     for k in range(2, n_groups):
         for j in range(1, GROUP):
             slot = column(jnp.bitwise_xor(group, k), jnp.bitwise_xor(place, j))
             handover(slot, near[j - 1])
+    pl.when(upper)(across_z)
     for r in sides:
         arrived(b_buf, b_recv, b_send, r, at(r=r))
         arrived(b_buf, b_recv, b_send, jnp.bitwise_xor(r, 1), at(r=r))
@@ -227,6 +268,17 @@
     for copy in started:
         copy.wait_send()
 
+    def sent(buf, slot, sem, target):
+        pltpu.make_async_remote_copy(
+            src_ref=buf.at[slot], dst_ref=buf.at[slot], send_sem=sem, recv_sem=sem, device_id=target, device_id_type=MESH
+        ).wait_send()
+
+    for k, c in enumerate(far):
+        sent(a_buf, col, f_send.at[k], at(c=c))
+    for i, r in enumerate(sides):
+        sent(b_buf, partner, b_send.at[len(sides) + i], at(r=r))
+    sent(b_buf, row, b_send.at[2 * len(sides)], at(r=partner))
+
 
 def body(factors, amplitudes, virt_irreps, win_irreps, occ_irreps, pair_list):
     n_rows, n_cols, n_pairs = (lax.axis_size(name) for name in ("row", "col", "pair"))
@@ -238,16 +290,23 @@
     n_groups = n_cols // 2 // GROUP
     n_x = n_rows // 2
     height = per_device * width
-    a_sends = (n_groups - 1) + n_groups * (GROUP - 1) + n_cols // 2
+    a_sends = n_groups * (GROUP - 1) + n_cols // 2
     b_sends = 1 + 2 * (n_x - 1)
-    vmem, smem = pl.BlockSpec(memory_space=pltpu.VMEM), pl.BlockSpec(memory_space=pltpu.SMEM)
+    hbm = pl.BlockSpec(memory_space=pltpu.HBM)
     dma = pltpu.SemaphoreType.DMA
     out = pl.pallas_call(
         functools.partial(kernel, (n_rows, n_cols, n_pairs, slab)),
         out_shape=jax.ShapeDtypeStruct((slab, n_b, n_a), jnp.float32),
-        in_specs=[vmem, vmem, smem, smem, smem, smem],
-        out_specs=vmem,
+        in_specs=[hbm] * 6,
+        out_specs=pl.BlockSpec(memory_space=pltpu.VMEM),
         scratch_shapes=[
+            pltpu.VMEM((per_device, width, factors.shape[0]), factors.dtype),
+            pltpu.VMEM(amplitudes.shape, amplitudes.dtype),
+            pltpu.SMEM(virt_irreps.shape, jnp.int32),
+            pltpu.SMEM(win_irreps.shape, jnp.int32),
+            pltpu.SMEM(occ_irreps.shape, jnp.int32),
+            pltpu.SMEM(pair_list.shape[::-1], jnp.int32),
+            dma((6,)),
             pltpu.VMEM((n_cols, height, LANES), jnp.bfloat16),
             pltpu.VMEM((n_rows, height, LANES), jnp.bfloat16),
             pltpu.VMEM((n_pairs, slab * width, width), jnp.bfloat16),
@@ -259,10 +318,10 @@
             dma((a_sends,)), dma((n_cols,)),
             dma((b_sends,)), dma((n_rows,)),
             dma((n_pairs,)), dma((n_pairs,)),
-            dma((n_pairs,)), dma((n_pairs,)),
+            dma((n_pairs,)), dma((n_pairs,)), dma((n_groups - 1,)),
         ],
         compiler_params=pltpu.CompilerParams(
-            collective_id=0, has_side_effects=True, vmem_limit_bytes=32 * 1024 * 1024
+            collective_id=0, has_side_effects=True, vmem_limit_bytes=56 * 1024 * 1024
         ),
         name="ladder",
     )(jnp.transpose(factors, (1, 2, 0)), amplitudes, virt_irreps, win_irreps, occ_irreps, pair_list.T)

time: 71.6 us -> 64.9 us (0.906)
  the two profiles are of different devices: /device:TPU:1 before, /device:TPU:984 now
where the time goes in v3:
time: 64.9 us; the launch traced here: 64.7 us
  Pallas kernels  63.1 us (97%)
  local copies, waits for them, and re-layouts  1.53 us (2%)
    pallas_call x1, Pallas kernels, body(): pl.pallas_call(functools.partial(kernel, (n_rows, n_cols, n_pairs, slab))...  63.1 us
    unnamed x1, local copies, waits for them, and re-layouts  1.53 us

profile of v3, /device:TPU:984, one launch (start us, length us, event | category | flops | bytes accessed | tf_op | source)
XLA Modules:
  0.0 64.7 jit_solution(15271119428107763646)
XLA Ops:
  0.0 63.1 %ladder.1 = f32[10,16,64]{2,1,0:T(8,128)} custom-call(bf16[2,16,450]{2,1,0:T(8,128)(2,1)} %bitcast.6, bf16[10,16,16]{2,1,0:T(8,128)(2,1)} %amp_hbm.1, s32[512]{0:T(512)} %virt_hbm.1, s32[16]{0:T(128)} %win_hbm.1, s32[120]{0:T(128)} %occ_hbm.1, s32[2,40]{1,0:T(2,128)} %bitcast.7), custom_call_target="tpu_custom_call" | custom-call | tf_op jit(solution)/shard_map/ladder/pallas_call | solution.py:297
  63.1 1.5 %copy.8 = f32[10,64,8,2]{1,3,2,0:T(2,128)} copy(f32[10,64,8,2]{1,3,2,0:T(2,128)} %bitcast.5) | data formatting | bytes 81920

commit v4 on v0

v4 whole, which is shorter than its diff:
```python
import functools

import jax
import jax.numpy as jnp
from jax import lax
from jax.experimental import pallas as pl
from jax.experimental.pallas import tpu as pltpu
from jax.sharding import PartitionSpec as P

MESH = pl.DeviceIdType.MESH
LANES = 512
GROUP = 4


def kernel(
    dims, x_hbm, amp_hbm, virt_hbm, win_hbm, occ_hbm, pairs_hbm, out_ref,
    x_ref, amp_ref, virt_ref, win_ref, occ_ref, pairs_ref, local,
    a_buf, b_buf, transit, w_buf, wide, integral, parts, sums, inbox,
    near_send, mate_send, chain_send, a_recv, side_send, cross_send, fan_send, cross_recv, b_recv,
    w_send, w_recv, r_send, r_recv,
):
    n_rows, n_cols, n_pairs, slab = dims
    row, col, pair = lax.axis_index("row"), lax.axis_index("col"), lax.axis_index("pair")
    width = amp_ref.shape[2]
    height = 2 * width
    n_fit = x_ref.shape[2]
    n_groups = n_cols // 2 // GROUP
    n_x = n_rows // 2
    core = lax.rem(col, 2)
    place = lax.rem(lax.div(col, 2), GROUP)
    group = lax.div(lax.div(col, 2), GROUP)
    upper = jnp.bitwise_and(row, 1) == 1

    def column(g, p):
        return (g * GROUP + p) * 2 + core

    def at(r=None, c=None, p=None):
        return (row if r is None else r, col if c is None else c, pair if p is None else p)

    near = [column(group, jnp.bitwise_xor(place, j)) for j in range(1, GROUP)]
    beside = near[0]
    mate = jnp.bitwise_xor(col, 1)
    half = jnp.bitwise_xor(row, 1)
    sides = [jnp.bitwise_xor(row, 2 * k) for k in range(1, n_x)]
    others = [jnp.bitwise_xor(pair, k) for k in range(1, n_pairs)]
    left, right = column(group - 1, place), column(group + 1, place)
    has_left, has_right = group > 0, group < n_groups - 1

    barrier = pltpu.get_barrier_semaphore()

    def greet(peer):
        pl.semaphore_signal(barrier, inc=1, device_id=peer, device_id_type=MESH)

    peers = [at(c=c) for c in near + [mate]] + [at(r=r) for r in sides] + [at(p=p) for p in others]
    peers += [at(r=r, c=beside) for r in sides]
    for peer in peers:
        greet(peer)
    pl.when(has_right)(lambda: greet(at(c=right)))
    pl.when(jnp.logical_not(upper))(lambda: greet(at(r=half, c=beside)))

    loads = []
    operands = (
        (x_hbm, x_ref), (amp_hbm, amp_ref), (win_hbm, win_ref), (occ_hbm, occ_ref), (pairs_hbm, pairs_ref),
        (virt_hbm, virt_ref),
    )
    for i, (src, dst) in enumerate(operands):
        loads.append(pltpu.make_async_copy(src, dst, local.at[i]))
        loads[i].start()

    loads[0].wait()
    own = jnp.concatenate([x_ref[0], x_ref[1]], axis=0)
    own = jnp.concatenate([own, jnp.zeros((height, LANES - n_fit), own.dtype)], axis=1)
    a_buf[col] = own
    b_buf[row] = own

    pl.semaphore_wait(barrier, len(peers) + jnp.where(has_left, 1, 0) + jnp.where(upper, 1, 0))

    def copy(src, dst, sent, landed, target):
        return pltpu.make_async_remote_copy(
            src_ref=src, dst_ref=dst, send_sem=sent, recv_sem=landed, device_id=target, device_id_type=MESH
        )

    def block(slot, sent, c):
        return copy(a_buf.at[slot], a_buf.at[slot], sent, a_recv.at[slot], at(c=c))

    def cross():
        return copy(a_buf.at[col], transit, cross_send, cross_recv, at(r=half, c=beside))

    def fan(i, r):
        return copy(transit, b_buf.at[half], fan_send.at[i], b_recv.at[half], at(r=r, c=beside))

    def side(i, r):
        return copy(b_buf.at[row], b_buf.at[row], side_send.at[i], b_recv.at[row], at(r=r))

    def near_copy(g, slot, j):
        return block(slot, near_send.at[g * (GROUP - 1) + j], near[j])

    def mate_copy(slot):
        return block(slot, mate_send.at[lax.div(slot, 2)], mate)

    def spread_block(g):
        slot = column(g, place)
        for j in range(GROUP - 1):
            near_copy(g, slot, j).start()
        mate_copy(slot).start()

    def chain(g, target, index):
        return block(column(g, place), chain_send.at[index], target)

    pl.when(upper)(lambda: cross().start())
    pl.when(has_left)(lambda: chain(group, left, n_groups).start())
    spread_block(group)
    for i, r in enumerate(sides):
        side(i, r).start()

    for load in loads[1:]:
        load.wait()
    symmetry = []
    for s in range(slab):
        first, second = pairs_ref[0, pair * slab + s], pairs_ref[1, pair * slab + s]
        symmetry.append(jnp.bitwise_xor(occ_ref[first], occ_ref[second]))
    down = lax.broadcasted_iota(jnp.int32, (width, width), 0)
    across = lax.broadcasted_iota(jnp.int32, (width, width), 1)
    product = jnp.zeros((width, width), jnp.int32)
    for j in range(width):
        label = win_ref[j]
        product = jnp.bitwise_xor(product, jnp.where(down == j, label, 0))
        product = jnp.bitwise_xor(product, jnp.where(across == j, label, 0))
    for s in range(slab):
        kept = jnp.where(product == symmetry[s], amp_ref[s].astype(jnp.float32), 0.0)
        w_buf[pair, s * width:(s + 1) * width, :] = kept.astype(jnp.bfloat16)

    def give_weights(i):
        return copy(w_buf.at[pair], w_buf.at[pair], w_send.at[i], w_recv.at[pair], at(p=others[i]))

    for i in range(len(others)):
        give_weights(i).start()

    n_b = n_x * 2
    span = n_b * width
    tall = slab * n_b
    line = lax.broadcasted_iota(jnp.int32, (2 * n_b, span), 0)
    lane = lax.broadcasted_iota(jnp.int32, (2 * n_b, span), 1)
    own_b = lax.div(lane, width) == lax.rem(line, n_b)
    spread = (
        lax.rem(lax.broadcasted_iota(jnp.int32, (width, span), 1), width)
        == lax.broadcasted_iota(jnp.int32, (width, span), 0)
    ).astype(jnp.bfloat16)

    def expand(p):
        def one(s, carry):
            lines = jnp.dot(
                w_buf[p, pl.ds(pl.multiple_of(s * 2 * width, 2 * width), 2 * width), :], spread,
                preferred_element_type=jnp.float32,
            )
            start = pl.multiple_of(p * tall + s * 2 * n_b, 2 * n_b)
            for c in range(width):
                first = jnp.broadcast_to(lines[c:c + 1, :], own_b.shape)
                second = jnp.broadcast_to(lines[width + c:width + c + 1, :], own_b.shape)
                tile = jnp.where(own_b, jnp.where(line < n_b, first, second), 0.0)
                wide[pl.ds(start, 2 * n_b), c * span:(c + 1) * span] = tile.astype(jnp.bfloat16)
            return carry

        lax.fori_loop(0, slab // 2, one, 0)

    expand(pair)

    def from_right(d):
        g = group + d
        block(column(g, place), chain_send.at[0], right).wait_recv()
        if d == 1:
            chain(group, right, n_groups + 1).start()
        pl.when(has_left)(lambda: chain(g, left, g).start())
        spread_block(g)

    def from_left(d):
        g = group - d
        block(column(g, place), chain_send.at[0], left).wait_recv()
        pl.when(has_right)(lambda: chain(g, right, g).start())
        spread_block(g)

    for d in range(1, n_groups):
        pl.when(group + d < n_groups)(functools.partial(from_right, d))
        pl.when(group - d >= 0)(functools.partial(from_left, d))
        if d == 1:
            for p in others:
                copy(w_buf.at[p], w_buf.at[p], w_send.at[0], w_recv.at[p], at(p=p)).wait_recv()
                expand(p)

    def handover(k, j):
        slot = column(jnp.bitwise_xor(group, k), jnp.bitwise_xor(place, j))
        block(slot, near_send.at[0], near[j - 1]).wait_recv()
        mate_copy(slot).start()

    def from_half():
        cross().wait_recv()
        pl.when(jnp.logical_not(upper))(lambda: cross().start())
        for i, r in enumerate([row] + sides):
            fan(i, r).start()

    for k in range(2):
        for j in range(1, GROUP):
            handover(k, j)
    pl.when(jnp.logical_not(upper))(from_half)
    for k in range(2, n_groups):
        for j in range(1, GROUP):
            handover(k, j)
    pl.when(upper)(from_half)
    for r in sides:
        copy(b_buf.at[r], b_buf.at[r], side_send.at[0], b_recv.at[r], at(r=r)).wait_recv()
    for c in range(n_cols // 2):
        block(2 * c + 1 - core, mate_send.at[0], mate).wait_recv()

    n_a = 2 * n_cols
    chunk = 8

    def contract(side_of, where):
        b_rows = jnp.concatenate([b_buf[2 * x + side_of] for x in range(n_x)], axis=0)

        def multiply(i, carry):
            first = pl.multiple_of(i * chunk, chunk)
            rows = a_buf[pl.ds(first, chunk)].reshape(chunk * height, LANES)
            integral[pl.ds(pl.multiple_of(first * height, chunk * height), chunk * height), :] = lax.dot_general(
                rows, b_rows, (((1,), (1,)), ((), ())), preferred_element_type=jnp.float32
            )
            return carry

        lax.fori_loop(0, n_cols // chunk, multiply, 0)
        for c in range(width):
            lines = integral[pl.ds(c, n_a, stride=width), :]
            high = lines.astype(jnp.bfloat16)
            parts[0:n_a, c * span:(c + 1) * span] = high
            parts[n_a:2 * n_a, c * span:(c + 1) * span] = (lines - high.astype(jnp.float32)).astype(jnp.bfloat16)

    def residual(p):
        both = lax.dot_general(
            wide[pl.ds(pl.multiple_of(p * tall, 2 * n_b), tall), :], parts[...], (((1,), (1,)), ((), ())),
            preferred_element_type=jnp.float32,
        )
        return both[:, 0:n_a] + both[:, n_a:2 * n_a]

    here = jnp.bitwise_and(row, 1)
    contract(here, 0)
    for p in others + [pair]:
        sums[p, :, 0:n_a] = residual(p)

    label_lane = lax.broadcasted_iota(jnp.int32, (n_b, 2 * n_a), 1)
    label_line = lax.broadcasted_iota(jnp.int32, (n_b, 2 * n_a), 0)
    label = jnp.zeros((n_b, 2 * n_a), jnp.int32)
    lane_a = lax.rem(label_lane, n_a)
    for j in range(n_a):
        label = jnp.where(lane_a == j, virt_ref[row * n_a + j], label)
    for x in range(n_x):
        for m in range(2):
            mine = virt_ref[(2 * x + here) * n_a + col * 2 + m]
            far = virt_ref[(2 * x + 1 - here) * n_a + col * 2 + m]
            there = jnp.where(label_lane < n_a, mine, far)
            label = jnp.bitwise_xor(label, jnp.where(label_line == 2 * x + m, there, 0))

    for i in range(n_x):
        r = jnp.bitwise_xor(half, 2 * i)
        copy(transit, b_buf.at[r], fan_send.at[0], b_recv.at[r], at(r=jnp.bitwise_xor(row, 2 * i), c=beside)).wait_recv()
    contract(1 - here, 1)

    def give_sum(i):
        return copy(sums.at[others[i]], inbox.at[pair], r_send.at[i], r_recv.at[pair], at(p=others[i]))

    for i, p in enumerate(others):
        sums[p, :, n_a:2 * n_a] = residual(p)
        give_sum(i).start()
    sums[pair, :, n_a:2 * n_a] = residual(pair)
    total = sums[pair]
    for p in others:
        copy(sums.at[p], inbox.at[p], r_send.at[0], r_recv.at[p], at(p=p)).wait_recv()
        total = total + inbox[p]
    for s in range(slab):
        kept = jnp.where(label == symmetry[s], total[s * n_b:(s + 1) * n_b], 0.0)
        mine, far = kept[:, 0:n_a], kept[:, n_a:2 * n_a]
        even, odd = jnp.where(upper, far, mine), jnp.where(upper, mine, far)
        for x in range(n_x):
            out_ref[s, 4 * x:4 * x + 2, :] = even[2 * x:2 * x + 2]
            out_ref[s, 4 * x + 2:4 * x + 4, :] = odd[2 * x:2 * x + 2]

    for g in range(n_groups):
        slot = column(g, place)
        for j in range(GROUP - 1):
            near_copy(g, slot, j).wait_send()
        pl.when(jnp.logical_or(jnp.logical_and(g > group, has_left), jnp.logical_and(g < group, has_right)))(
            functools.partial(lambda g: chain(g, left, g).wait_send(), g)
        )
    pl.when(has_left)(lambda: chain(group, left, n_groups).wait_send())
    pl.when(has_right)(lambda: chain(group, right, n_groups + 1).wait_send())
    for c in range(n_cols // 2):
        mate_copy(2 * c + core).wait_send()
    for i, r in enumerate(sides):
        side(i, r).wait_send()
    for i, r in enumerate([row] + sides):
        fan(i, r).wait_send()
    cross().wait_send()
    for i in range(len(others)):
        give_weights(i).wait_send()
        give_sum(i).wait_send()


def body(factors, amplitudes, virt_irreps, win_irreps, occ_irreps, pair_list):
    n_rows, n_cols, n_pairs = (lax.axis_size(name) for name in ("row", "col", "pair"))
    slab, width = amplitudes.shape[0], amplitudes.shape[1]
    per_device = factors.shape[1]
    n_a = per_device * n_cols
    n_x = n_rows // 2
    n_b = n_x * per_device
    span = n_b * width
    n_groups = n_cols // 2 // GROUP
    height = per_device * width
    hbm = pl.BlockSpec(memory_space=pltpu.HBM)
    dma = pltpu.SemaphoreType.DMA
    out = pl.pallas_call(
        functools.partial(kernel, (n_rows, n_cols, n_pairs, slab)),
        out_shape=jax.ShapeDtypeStruct((slab, n_rows * per_device, n_a), jnp.float32),
        in_specs=[hbm] * 6,
        out_specs=pl.BlockSpec(memory_space=pltpu.VMEM),
        scratch_shapes=[
            pltpu.VMEM((per_device, width, factors.shape[0]), factors.dtype),
            pltpu.VMEM(amplitudes.shape, amplitudes.dtype),
            pltpu.SMEM(virt_irreps.shape, jnp.int32),
            pltpu.SMEM(win_irreps.shape, jnp.int32),
            pltpu.SMEM(occ_irreps.shape, jnp.int32),
            pltpu.SMEM(pair_list.shape[::-1], jnp.int32),
            dma((6,)),
            pltpu.VMEM((n_cols, height, LANES), jnp.bfloat16),
            pltpu.VMEM((n_rows, height, LANES), jnp.bfloat16),
            pltpu.VMEM((height, LANES), jnp.bfloat16),
            pltpu.VMEM((n_pairs, slab * width, width), jnp.bfloat16),
            pltpu.VMEM((n_pairs * slab * n_b, width * span), jnp.bfloat16),
            pltpu.VMEM((n_a * width, span), jnp.float32),
            pltpu.VMEM((2 * n_a, width * span), jnp.bfloat16),
            pltpu.VMEM((n_pairs, slab * n_b, 2 * n_a), jnp.float32),
            pltpu.VMEM((n_pairs, slab * n_b, 2 * n_a), jnp.float32),
            dma((n_groups * (GROUP - 1),)), dma((n_cols // 2,)), dma((n_groups + 2,)), dma((n_cols,)),
            dma((n_x - 1,)), dma, dma((n_x,)), dma, dma((n_rows,)),
            dma((n_pairs,)), dma((n_pairs,)), dma((n_pairs,)), dma((n_pairs,)),
        ],
        compiler_params=pltpu.CompilerParams(
            collective_id=0, has_side_effects=True, vmem_limit_bytes=56 * 1024 * 1024
        ),
        name="ladder",
    )(jnp.transpose(factors, (1, 2, 0)), amplitudes, virt_irreps, win_irreps, occ_irreps, pair_list.T)
    return jnp.transpose(out.reshape(slab, n_rows, per_device, n_a), (0, 3, 1, 2))


def solution(mesh):
    in_specs = (P("pair", ("row", "col"), None), P("pair", None, None), P(), P(), P(), P())
    out_specs = P("pair", "row", None, "col")
    return jax.shard_map(body, mesh=mesh, in_specs=in_specs, out_specs=out_specs, check_vma=False)
```

time: 429 us -> 59.7 us (0.14)
  the two profiles are of different devices: /device:TPU:4 before, /device:TPU:1 now
where the time goes in v4:
time: 59.7 us; the launch traced here: 59.5 us
  Pallas kernels  58 us (97%)
  local copies, waits for them, and re-layouts  1.53 us (3%)
    pallas_call x1, Pallas kernels, body(): pl.pallas_call(functools.partial(kernel, (n_rows, n_cols, n_pairs, slab))...  58 us
    unnamed x1, local copies, waits for them, and re-layouts  1.53 us

profile of v4, /device:TPU:1, one launch (start us, length us, event | category | flops | bytes accessed | tf_op | source)
XLA Modules:
  0.0 59.5 jit_solution(4094398408478612097)
XLA Ops:
  0.0 58.0 %ladder.1 = f32[10,16,64]{2,1,0:T(8,128)} custom-call(bf16[2,16,450]{2,1,0:T(8,128)(2,1)} %bitcast.6, bf16[10,16,16]{2,1,0:T(8,128)(2,1)} %amp_hbm.1, s32[512]{0:T(512)} %virt_hbm.1, s32[16]{0:T(128)} %win_hbm.1, s32[120]{0:T(128)} %occ_hbm.1, s32[2,40]{1,0:T(2,128)} %bitcast.7), custom_call_target="tpu_custom_call" | custom-call | tf_op jit(solution)/shard_map/ladder/pallas_call | solution.py:317
  58.0 1.5 %copy.8 = f32[10,64,8,2]{1,3,2,0:T(2,128)} copy(f32[10,64,8,2]{1,3,2,0:T(2,128)} %bitcast.5) | data formatting | bytes 81920

commit v5 on v4

--- a/solution.py
+++ b/solution.py
@@ -17,7 +17,7 @@
     x_ref, amp_ref, virt_ref, win_ref, occ_ref, pairs_ref, local,
     a_buf, b_buf, transit, w_buf, wide, integral, parts, sums, inbox,
     near_send, mate_send, chain_send, a_recv, side_send, cross_send, fan_send, cross_recv, b_recv,
-    w_send, w_recv, r_send, r_recv,
+    w_send, w_recv, r_send, r_recv, edge_send, ready,
 ):
     n_rows, n_cols, n_pairs, slab = dims
     row, col, pair = lax.axis_index("row"), lax.axis_index("col"), lax.axis_index("pair")
@@ -45,6 +45,14 @@
     others = [jnp.bitwise_xor(pair, k) for k in range(1, n_pairs)]
     left, right = column(group - 1, place), column(group + 1, place)
     has_left, has_right = group > 0, group < n_groups - 1
+    lower = jnp.logical_not(upper)
+    at_first, at_last = jnp.logical_not(has_left), jnp.logical_not(has_right)
+    direct_out = jnp.logical_and(upper, has_right)
+    direct_in = jnp.logical_and(lower, has_right)
+    edge = jnp.logical_or(at_first, at_last)
+    low_edge, high_edge = jnp.logical_and(lower, edge), jnp.logical_and(upper, edge)
+    opposite = column(n_groups - 1 - group, place)
+    inner = jnp.where(at_first, column(1, place), column(n_groups - 2, place))
 
     barrier = pltpu.get_barrier_semaphore()
 
@@ -56,7 +64,9 @@
     for peer in peers:
         greet(peer)
     pl.when(has_right)(lambda: greet(at(c=right)))
-    pl.when(jnp.logical_not(upper))(lambda: greet(at(r=half, c=beside)))
+    pl.when(jnp.logical_and(upper, has_left))(lambda: greet(at(c=left)))
+    pl.when(low_edge)(lambda: greet(at(r=half, c=opposite)))
+    pl.when(direct_in)(lambda: greet(at(r=half, c=beside)))
 
     loads = []
     operands = (
@@ -73,7 +83,11 @@
     a_buf[col] = own
     b_buf[row] = own
 
-    pl.semaphore_wait(barrier, len(peers) + jnp.where(has_left, 1, 0) + jnp.where(upper, 1, 0))
+    awaited = len(peers) + jnp.where(has_left, 1, 0) + jnp.where(direct_out, 2, 0) + jnp.where(high_edge, 1, 0)
+    pl.semaphore_wait(barrier, awaited)
+    pl.when(high_edge)(
+        lambda: pl.semaphore_signal(ready, inc=1, device_id=at(r=half, c=opposite), device_id_type=MESH)
+    )
 
     def copy(src, dst, sent, landed, target):
         return pltpu.make_async_remote_copy(
@@ -88,6 +102,18 @@
 
     def fan(i, r):
         return copy(transit, b_buf.at[half], fan_send.at[i], b_recv.at[half], at(r=r, c=beside))
+
+    def over(source, to_b, index):
+        return copy(
+            a_buf.at[source], b_buf.at[row] if to_b else transit, edge_send.at[index],
+            b_recv.at[row] if to_b else cross_recv, at(r=half, c=opposite),
+        )
+
+    def inward():
+        return copy(transit, b_buf.at[half], edge_send.at[0], b_recv.at[half], at(c=inner))
+
+    def share(i, r):
+        return copy(b_buf.at[half], b_buf.at[half], fan_send.at[i + 1], b_recv.at[half], at(r=r))
 
     def side(i, r):
         return copy(b_buf.at[row], b_buf.at[row], side_send.at[i], b_recv.at[row], at(r=r))
@@ -107,8 +133,9 @@
     def chain(g, target, index):
         return block(column(g, place), chain_send.at[index], target)
 
-    pl.when(upper)(lambda: cross().start())
+    pl.when(direct_out)(lambda: cross().start())
     pl.when(has_left)(lambda: chain(group, left, n_groups).start())
+    pl.when(jnp.logical_and(upper, has_right))(lambda: chain(group, right, n_groups + 1).start())
     spread_block(group)
     for i, r in enumerate(sides):
         side(i, r).start()
@@ -165,18 +192,29 @@
 
     expand(pair)
 
+    def onward(d, g):
+        if d == n_groups - 2:
+            pl.semaphore_wait(ready, 1)
+        over(column(g, place), d == n_groups - 1, d - (n_groups - 2)).start()
+
     def from_right(d):
         g = group + d
         block(column(g, place), chain_send.at[0], right).wait_recv()
         if d == 1:
-            chain(group, right, n_groups + 1).start()
+            pl.when(lower)(lambda: chain(group, right, n_groups + 1).start())
         pl.when(has_left)(lambda: chain(g, left, g).start())
+        if d >= n_groups - 2:
+            pl.when(jnp.logical_and(at_first, lower))(lambda: onward(d, g))
+        if d == n_groups - 1:
+            pl.when(jnp.logical_and(upper, at_first))(lambda: over(column(g, place), True, 1).start())
         spread_block(g)
 
     def from_left(d):
         g = group - d
         block(column(g, place), chain_send.at[0], left).wait_recv()
         pl.when(has_right)(lambda: chain(g, right, g).start())
+        if d >= n_groups - 2:
+            pl.when(jnp.logical_and(at_last, lower))(lambda: onward(d, g))
         spread_block(g)
 
     for d in range(1, n_groups):
@@ -192,20 +230,26 @@
         block(slot, near_send.at[0], near[j - 1]).wait_recv()
         mate_copy(slot).start()
 
-    def from_half():
+    def turn_in():
         cross().wait_recv()
-        pl.when(jnp.logical_not(upper))(lambda: cross().start())
+        inward().start()
+
+    def from_direct():
+        cross().wait_recv()
         for i, r in enumerate([row] + sides):
             fan(i, r).start()
 
-    for k in range(2):
+    def from_chain():
+        share(0, row).wait_recv()
+        for i, r in enumerate(sides):
+            share(i, r).start()
+
+    pl.when(high_edge)(turn_in)
+    pl.when(direct_in)(from_direct)
+    for k in range(n_groups):
         for j in range(1, GROUP):
             handover(k, j)
-    pl.when(jnp.logical_not(upper))(from_half)
-    for k in range(2, n_groups):
-        for j in range(1, GROUP):
-            handover(k, j)
-    pl.when(upper)(from_half)
+    pl.when(jnp.logical_not(direct_in))(from_chain)
     for r in sides:
         copy(b_buf.at[r], b_buf.at[r], side_send.at[0], b_recv.at[r], at(r=r)).wait_recv()
     for c in range(n_cols // 2):
@@ -257,9 +301,13 @@
             there = jnp.where(label_lane < n_a, mine, far)
             label = jnp.bitwise_xor(label, jnp.where(label_line == 2 * x + m, there, 0))
 
-    for i in range(n_x):
-        r = jnp.bitwise_xor(half, 2 * i)
-        copy(transit, b_buf.at[r], fan_send.at[0], b_recv.at[r], at(r=jnp.bitwise_xor(row, 2 * i), c=beside)).wait_recv()
+    def half_arrived(i):
+        slot = jnp.bitwise_xor(half, 2 * i)
+        copy(b_buf.at[slot], b_buf.at[slot], fan_send.at[0], b_recv.at[slot], at(r=half, c=beside)).wait_recv()
+
+    pl.when(direct_in)(lambda: half_arrived(0))
+    for i in range(1, n_x):
+        half_arrived(i)
     contract(1 - here, 1)
 
     def give_sum(i):
@@ -294,9 +342,14 @@
         mate_copy(2 * c + core).wait_send()
     for i, r in enumerate(sides):
         side(i, r).wait_send()
-    for i, r in enumerate([row] + sides):
-        fan(i, r).wait_send()
-    cross().wait_send()
+    pl.when(direct_in)(lambda: fan(0, row).wait_send())
+    for i, r in enumerate(sides):
+        share(i, r).wait_send()
+    pl.when(direct_out)(lambda: cross().wait_send())
+    pl.when(low_edge)(lambda: over(col, False, 0).wait_send())
+    pl.when(low_edge)(lambda: over(col, True, 1).wait_send())
+    pl.when(jnp.logical_and(upper, at_first))(lambda: over(col, True, 1).wait_send())
+    pl.when(high_edge)(lambda: inward().wait_send())
     for i in range(len(others)):
         give_weights(i).wait_send()
         give_sum(i).wait_send()
@@ -338,7 +391,8 @@
             pltpu.VMEM((n_pairs, slab * n_b, 2 * n_a), jnp.float32),
             dma((n_groups * (GROUP - 1),)), dma((n_cols // 2,)), dma((n_groups + 2,)), dma((n_cols,)),
             dma((n_x - 1,)), dma, dma((n_x,)), dma, dma((n_rows,)),
-            dma((n_pairs,)), dma((n_pairs,)), dma((n_pairs,)), dma((n_pairs,)),
+            dma((n_pairs,)), dma((n_pairs,)), dma((n_pairs,)), dma((n_pairs,)), dma((2,)),
+            pltpu.SemaphoreType.REGULAR,
         ],
         compiler_params=pltpu.CompilerParams(
             collective_id=0, has_side_effects=True, vmem_limit_bytes=56 * 1024 * 1024

time: 59.7 us -> 59 us (0.988)
  Pallas kernels: 58 us -> 57.2 us
    pallas_call x1, Pallas kernels: 58 us -> 57.2 us  [body(): pl.pallas_call(functools.partial(kernel, (n_rows, n_cols, n_pairs, slab))...]
where the time goes in v5:
time: 59 us; the launch traced here: 58.8 us
  Pallas kernels  57.2 us (97%)
  local copies, waits for them, and re-layouts  1.53 us (3%)
    pallas_call x1, Pallas kernels, body(): pl.pallas_call(functools.partial(kernel, (n_rows, n_cols, n_pairs, slab))...  57.2 us
    unnamed x1, local copies, waits for them, and re-layouts  1.53 us

profile of v5, /device:TPU:1, one launch (start us, length us, event | category | flops | bytes accessed | tf_op | source)
XLA Modules:
  0.0 58.8 jit_solution(10983123401791251300)
XLA Ops:
  0.0 57.2 %ladder.1 = f32[10,16,64]{2,1,0:T(8,128)} custom-call(bf16[2,16,450]{2,1,0:T(8,128)(2,1)} %bitcast.6, bf16[10,16,16]{2,1,0:T(8,128)(2,1)} %amp_hbm.1, s32[512]{0:T(512)} %virt_hbm.1, s32[16]{0:T(128)} %win_hbm.1, s32[120]{0:T(128)} %occ_hbm.1, s32[2,40]{1,0:T(2,128)} %bitcast.7), custom_call_target="tpu_custom_call" | custom-call | tf_op jit(solution)/shard_map/ladder/pallas_call | solution.py:370
  57.2 1.5 %copy.8 = f32[10,64,8,2]{1,3,2,0:T(2,128)} copy(f32[10,64,8,2]{1,3,2,0:T(2,128)} %bitcast.5) | data formatting | bytes 81920

commit v6 on v5

--- a/solution.py
+++ b/solution.py
@@ -51,6 +51,8 @@
     direct_in = jnp.logical_and(lower, has_right)
     edge = jnp.logical_or(at_first, at_last)
     low_edge, high_edge = jnp.logical_and(lower, edge), jnp.logical_and(upper, edge)
+    leap = jnp.logical_and(lower, group >= 2)
+    passes_left = jnp.logical_and(has_left, jnp.logical_or(upper, group >= 2))
     opposite = column(n_groups - 1 - group, place)
     inner = jnp.where(at_first, column(1, place), column(n_groups - 2, place))
 
@@ -65,6 +67,8 @@
         greet(peer)
     pl.when(has_right)(lambda: greet(at(c=right)))
     pl.when(jnp.logical_and(upper, has_left))(lambda: greet(at(c=left)))
+    for g in range(2, n_groups):
+        pl.when(jnp.logical_and(lower, at_first))(functools.partial(greet, at(c=column(g, place))))
     pl.when(low_edge)(lambda: greet(at(r=half, c=opposite)))
     pl.when(direct_in)(lambda: greet(at(r=half, c=beside)))
 
@@ -84,6 +88,7 @@
     b_buf[row] = own
 
     awaited = len(peers) + jnp.where(has_left, 1, 0) + jnp.where(direct_out, 2, 0) + jnp.where(high_edge, 1, 0)
+    awaited = awaited + jnp.where(leap, 1, 0)
     pl.semaphore_wait(barrier, awaited)
     pl.when(high_edge)(
         lambda: pl.semaphore_signal(ready, inc=1, device_id=at(r=half, c=opposite), device_id_type=MESH)
@@ -134,6 +139,7 @@
         return block(column(g, place), chain_send.at[index], target)
 
     pl.when(direct_out)(lambda: cross().start())
+    pl.when(leap)(lambda: chain(group, column(0, place), n_groups + 2).start())
     pl.when(has_left)(lambda: chain(group, left, n_groups).start())
     pl.when(jnp.logical_and(upper, has_right))(lambda: chain(group, right, n_groups + 1).start())
     spread_block(group)
@@ -202,7 +208,7 @@
         block(column(g, place), chain_send.at[0], right).wait_recv()
         if d == 1:
             pl.when(lower)(lambda: chain(group, right, n_groups + 1).start())
-        pl.when(has_left)(lambda: chain(g, left, g).start())
+        pl.when(passes_left)(lambda: chain(g, left, g).start())
         if d >= n_groups - 2:
             pl.when(jnp.logical_and(at_first, lower))(lambda: onward(d, g))
         if d == n_groups - 1:
@@ -252,42 +258,8 @@
     pl.when(jnp.logical_not(direct_in))(from_chain)
     for r in sides:
         copy(b_buf.at[r], b_buf.at[r], side_send.at[0], b_recv.at[r], at(r=r)).wait_recv()
-    for c in range(n_cols // 2):
-        block(2 * c + 1 - core, mate_send.at[0], mate).wait_recv()
-
+    here = jnp.bitwise_and(row, 1)
     n_a = 2 * n_cols
-    chunk = 8
-
-    def contract(side_of, where):
-        b_rows = jnp.concatenate([b_buf[2 * x + side_of] for x in range(n_x)], axis=0)
-
-        def multiply(i, carry):
-            first = pl.multiple_of(i * chunk, chunk)
-            rows = a_buf[pl.ds(first, chunk)].reshape(chunk * height, LANES)
-            integral[pl.ds(pl.multiple_of(first * height, chunk * height), chunk * height), :] = lax.dot_general(
-                rows, b_rows, (((1,), (1,)), ((), ())), preferred_element_type=jnp.float32
-            )
-            return carry
-
-        lax.fori_loop(0, n_cols // chunk, multiply, 0)
-        for c in range(width):
-            lines = integral[pl.ds(c, n_a, stride=width), :]
-            high = lines.astype(jnp.bfloat16)
-            parts[0:n_a, c * span:(c + 1) * span] = high
-            parts[n_a:2 * n_a, c * span:(c + 1) * span] = (lines - high.astype(jnp.float32)).astype(jnp.bfloat16)
-
-    def residual(p):
-        both = lax.dot_general(
-            wide[pl.ds(pl.multiple_of(p * tall, 2 * n_b), tall), :], parts[...], (((1,), (1,)), ((), ())),
-            preferred_element_type=jnp.float32,
-        )
-        return both[:, 0:n_a] + both[:, n_a:2 * n_a]
-
-    here = jnp.bitwise_and(row, 1)
-    contract(here, 0)
-    for p in others + [pair]:
-        sums[p, :, 0:n_a] = residual(p)
-
     label_lane = lax.broadcasted_iota(jnp.int32, (n_b, 2 * n_a), 1)
     label_line = lax.broadcasted_iota(jnp.int32, (n_b, 2 * n_a), 0)
     label = jnp.zeros((n_b, 2 * n_a), jnp.int32)
@@ -308,16 +280,46 @@
     pl.when(direct_in)(lambda: half_arrived(0))
     for i in range(1, n_x):
         half_arrived(i)
-    contract(1 - here, 1)
+    b_rows = jnp.concatenate(
+        [b_buf[2 * x + here] for x in range(n_x)] + [b_buf[2 * x + 1 - here] for x in range(n_x)], axis=0
+    )
+    deep = 2 * GROUP * height
+    a_part = 2 * GROUP * 2
+
+    def contract(k):
+        g = jnp.bitwise_xor(group, k)
+        for p in range(GROUP):
+            slot = (g * GROUP + p) * 2 + 1 - core
+            block(slot, mate_send.at[0], mate).wait_recv()
+        rows = a_buf[pl.ds(pl.multiple_of(g * 2 * GROUP, 2 * GROUP), 2 * GROUP)].reshape(deep, LANES)
+        tile = lax.dot_general(rows, b_rows, (((1,), (1,)), ((), ())), preferred_element_type=jnp.float32)
+        for t in range(2):
+            integral[t] = tile[:, t * span:(t + 1) * span]
+            start = pl.multiple_of(t * n_a + g * a_part, a_part)
+            for c in range(width):
+                lines = integral[t, pl.ds(c, a_part, stride=width), :]
+                high = lines.astype(jnp.bfloat16)
+                low = (lines - high.astype(jnp.float32)).astype(jnp.bfloat16)
+                parts[pl.ds(start, a_part), c * span:(c + 1) * span] = high
+                parts[pl.ds(pl.multiple_of(2 * n_a + start, a_part), a_part), c * span:(c + 1) * span] = low
+
+    for k in range(n_groups):
+        contract(k)
+
+    def residual(p):
+        both = lax.dot_general(
+            wide[pl.ds(pl.multiple_of(p * tall, 2 * n_b), tall), :], parts[...], (((1,), (1,)), ((), ())),
+            preferred_element_type=jnp.float32,
+        )
+        return both[:, 0:2 * n_a] + both[:, 2 * n_a:4 * n_a]
 
     def give_sum(i):
         return copy(sums.at[others[i]], inbox.at[pair], r_send.at[i], r_recv.at[pair], at(p=others[i]))
 
     for i, p in enumerate(others):
-        sums[p, :, n_a:2 * n_a] = residual(p)
+        sums[p] = residual(p)
         give_sum(i).start()
-    sums[pair, :, n_a:2 * n_a] = residual(pair)
-    total = sums[pair]
+    total = residual(pair)
     for p in others:
         copy(sums.at[p], inbox.at[p], r_send.at[0], r_recv.at[p], at(p=p)).wait_recv()
         total = total + inbox[p]
@@ -333,10 +335,11 @@
         slot = column(g, place)
         for j in range(GROUP - 1):
             near_copy(g, slot, j).wait_send()
-        pl.when(jnp.logical_or(jnp.logical_and(g > group, has_left), jnp.logical_and(g < group, has_right)))(
+        pl.when(jnp.logical_or(jnp.logical_and(g > group, passes_left), jnp.logical_and(g < group, has_right)))(
             functools.partial(lambda g: chain(g, left, g).wait_send(), g)
         )
     pl.when(has_left)(lambda: chain(group, left, n_groups).wait_send())
+    pl.when(leap)(lambda: chain(group, left, n_groups + 2).wait_send())
     pl.when(has_right)(lambda: chain(group, right, n_groups + 1).wait_send())
     for c in range(n_cols // 2):
         mate_copy(2 * c + core).wait_send()
@@ -385,11 +388,11 @@
             pltpu.VMEM((height, LANES), jnp.bfloat16),
             pltpu.VMEM((n_pairs, slab * width, width), jnp.bfloat16),
             pltpu.VMEM((n_pairs * slab * n_b, width * span), jnp.bfloat16),
-            pltpu.VMEM((n_a * width, span), jnp.float32),
-            pltpu.VMEM((2 * n_a, width * span), jnp.bfloat16),
+            pltpu.VMEM((2, 2 * GROUP * height, span), jnp.float32),
+            pltpu.VMEM((4 * n_a, width * span), jnp.bfloat16),
             pltpu.VMEM((n_pairs, slab * n_b, 2 * n_a), jnp.float32),
             pltpu.VMEM((n_pairs, slab * n_b, 2 * n_a), jnp.float32),
-            dma((n_groups * (GROUP - 1),)), dma((n_cols // 2,)), dma((n_groups + 2,)), dma((n_cols,)),
+            dma((n_groups * (GROUP - 1),)), dma((n_cols // 2,)), dma((n_groups + 3,)), dma((n_cols,)),
             dma((n_x - 1,)), dma, dma((n_x,)), dma, dma((n_rows,)),
             dma((n_pairs,)), dma((n_pairs,)), dma((n_pairs,)), dma((n_pairs,)), dma((2,)),
             pltpu.SemaphoreType.REGULAR,

time: 59 us -> 51.8 us (0.88)
  Pallas kernels: 57.2 us -> 49.8 us
    pallas_call x1, Pallas kernels: 57.2 us -> 49.8 us  [body(): pl.pallas_call(functools.partial(kernel, (n_rows, n_cols, n_pairs, slab))...]
where the time goes in v6:
time: 51.8 us; the launch traced here: 51.3 us
  Pallas kernels  49.8 us (96%)
  local copies, waits for them, and re-layouts  1.53 us (3%)
    pallas_call x1, Pallas kernels, body(): pl.pallas_call(functools.partial(kernel, (n_rows, n_cols, n_pairs, slab))...  49.8 us
    unnamed x1, local copies, waits for them, and re-layouts  1.53 us

profile of v6, /device:TPU:1, one launch (start us, length us, event | category | flops | bytes accessed | tf_op | source)
XLA Modules:
  0.0 51.3 jit_solution(10771624408593659450)
XLA Ops:
  0.0 49.8 %ladder.1 = f32[10,16,64]{2,1,0:T(8,128)} custom-call(bf16[2,16,450]{2,1,0:T(8,128)(2,1)} %bitcast.6, bf16[10,16,16]{2,1,0:T(8,128)(2,1)} %amp_hbm.1, s32[512]{0:T(512)} %virt_hbm.1, s32[16]{0:T(128)} %win_hbm.1, s32[120]{0:T(128)} %occ_hbm.1, s32[2,40]{1,0:T(2,128)} %bitcast.7), custom_call_target="tpu_custom_call" | custom-call | tf_op jit(solution)/shard_map/ladder/pallas_call | solution.py:373
  49.8 1.5 %copy.8 = f32[10,64,8,2]{1,3,2,0:T(2,128)} copy(f32[10,64,8,2]{1,3,2,0:T(2,128)} %bitcast.5) | data formatting | bytes 81920

commit v7 on v6

--- a/solution.py
+++ b/solution.py
@@ -54,7 +54,9 @@
     leap = jnp.logical_and(lower, group >= 2)
     passes_left = jnp.logical_and(has_left, jnp.logical_or(upper, group >= 2))
     opposite = column(n_groups - 1 - group, place)
-    inner = jnp.where(at_first, column(1, place), column(n_groups - 2, place))
+    inner = jnp.where(at_first, column(n_groups - 2, place), column(1, place))
+    middle = jnp.logical_and(upper, jnp.logical_not(edge))
+    outer = jnp.where(group == 1, column(n_groups - 1, place), column(0, place))
 
     barrier = pltpu.get_barrier_semaphore()
 
@@ -70,6 +72,7 @@
     for g in range(2, n_groups):
         pl.when(jnp.logical_and(lower, at_first))(functools.partial(greet, at(c=column(g, place))))
     pl.when(low_edge)(lambda: greet(at(r=half, c=opposite)))
+    pl.when(low_edge)(lambda: greet(at(r=half, c=inner)))
     pl.when(direct_in)(lambda: greet(at(r=half, c=beside)))
 
     loads = []
@@ -87,11 +90,14 @@
     a_buf[col] = own
     b_buf[row] = own
 
-    awaited = len(peers) + jnp.where(has_left, 1, 0) + jnp.where(direct_out, 2, 0) + jnp.where(high_edge, 1, 0)
+    awaited = len(peers) + jnp.where(has_left, 1, 0) + jnp.where(direct_out, 2, 0) + jnp.where(upper, 1, 0)
     awaited = awaited + jnp.where(leap, 1, 0)
     pl.semaphore_wait(barrier, awaited)
     pl.when(high_edge)(
-        lambda: pl.semaphore_signal(ready, inc=1, device_id=at(r=half, c=opposite), device_id_type=MESH)
+        lambda: pl.semaphore_signal(ready.at[1], inc=1, device_id=at(r=half, c=opposite), device_id_type=MESH)
+    )
+    pl.when(middle)(
+        lambda: pl.semaphore_signal(ready.at[0], inc=1, device_id=at(r=half, c=outer), device_id_type=MESH)
     )
 
     def copy(src, dst, sent, landed, target):
@@ -108,14 +114,11 @@
     def fan(i, r):
         return copy(transit, b_buf.at[half], fan_send.at[i], b_recv.at[half], at(r=r, c=beside))
 
-    def over(source, to_b, index):
+    def over(source, index):
         return copy(
-            a_buf.at[source], b_buf.at[row] if to_b else transit, edge_send.at[index],
-            b_recv.at[row] if to_b else cross_recv, at(r=half, c=opposite),
+            a_buf.at[source], b_buf.at[row], edge_send.at[index], b_recv.at[row],
+            at(r=half, c=opposite if index else inner),
         )
-
-    def inward():
-        return copy(transit, b_buf.at[half], edge_send.at[0], b_recv.at[half], at(c=inner))
 
     def share(i, r):
         return copy(b_buf.at[half], b_buf.at[half], fan_send.at[i + 1], b_recv.at[half], at(r=r))
@@ -198,10 +201,11 @@
 
     expand(pair)
 
-    def onward(d, g):
-        if d == n_groups - 2:
-            pl.semaphore_wait(ready, 1)
-        over(column(g, place), d == n_groups - 1, d - (n_groups - 2)).start()
+    def onward():
+        for d in range(n_groups - 2, n_groups):
+            g = jnp.where(at_first, group + d, group - d)
+            pl.semaphore_wait(ready.at[d - (n_groups - 2)], 1)
+            over(column(g, place), d - (n_groups - 2)).start()
 
     def from_right(d):
         g = group + d
@@ -209,18 +213,14 @@
         if d == 1:
             pl.when(lower)(lambda: chain(group, right, n_groups + 1).start())
         pl.when(passes_left)(lambda: chain(g, left, g).start())
-        if d >= n_groups - 2:
-            pl.when(jnp.logical_and(at_first, lower))(lambda: onward(d, g))
         if d == n_groups - 1:
-            pl.when(jnp.logical_and(upper, at_first))(lambda: over(column(g, place), True, 1).start())
+            pl.when(jnp.logical_and(upper, at_first))(lambda: over(column(g, place), 1).start())
         spread_block(g)
 
     def from_left(d):
         g = group - d
         block(column(g, place), chain_send.at[0], left).wait_recv()
         pl.when(has_right)(lambda: chain(g, right, g).start())
-        if d >= n_groups - 2:
-            pl.when(jnp.logical_and(at_last, lower))(lambda: onward(d, g))
         spread_block(g)
 
     for d in range(1, n_groups):
@@ -236,10 +236,6 @@
         block(slot, near_send.at[0], near[j - 1]).wait_recv()
         mate_copy(slot).start()
 
-    def turn_in():
-        cross().wait_recv()
-        inward().start()
-
     def from_direct():
         cross().wait_recv()
         for i, r in enumerate([row] + sides):
@@ -250,12 +246,13 @@
         for i, r in enumerate(sides):
             share(i, r).start()
 
-    pl.when(high_edge)(turn_in)
+    pl.when(low_edge)(onward)
+    pl.when(upper)(from_chain)
     pl.when(direct_in)(from_direct)
     for k in range(n_groups):
         for j in range(1, GROUP):
             handover(k, j)
-    pl.when(jnp.logical_not(direct_in))(from_chain)
+    pl.when(jnp.logical_and(lower, at_last))(from_chain)
     for r in sides:
         copy(b_buf.at[r], b_buf.at[r], side_send.at[0], b_recv.at[r], at(r=r)).wait_recv()
     here = jnp.bitwise_and(row, 1)
@@ -283,6 +280,7 @@
     b_rows = jnp.concatenate(
         [b_buf[2 * x + here] for x in range(n_x)] + [b_buf[2 * x + 1 - here] for x in range(n_x)], axis=0
     )
+    b_rows = jnp.transpose(b_rows)
     deep = 2 * GROUP * height
     a_part = 2 * GROUP * 2
 
@@ -292,7 +290,7 @@
             slot = (g * GROUP + p) * 2 + 1 - core
             block(slot, mate_send.at[0], mate).wait_recv()
         rows = a_buf[pl.ds(pl.multiple_of(g * 2 * GROUP, 2 * GROUP), 2 * GROUP)].reshape(deep, LANES)
-        tile = lax.dot_general(rows, b_rows, (((1,), (1,)), ((), ())), preferred_element_type=jnp.float32)
+        tile = jnp.dot(rows, b_rows, preferred_element_type=jnp.float32)
         for t in range(2):
             integral[t] = tile[:, t * span:(t + 1) * span]
             start = pl.multiple_of(t * n_a + g * a_part, a_part)
@@ -306,20 +304,15 @@
     for k in range(n_groups):
         contract(k)
 
-    def residual(p):
-        both = lax.dot_general(
-            wide[pl.ds(pl.multiple_of(p * tall, 2 * n_b), tall), :], parts[...], (((1,), (1,)), ((), ())),
-            preferred_element_type=jnp.float32,
-        )
-        return both[:, 0:2 * n_a] + both[:, 2 * n_a:4 * n_a]
-
     def give_sum(i):
         return copy(sums.at[others[i]], inbox.at[pair], r_send.at[i], r_recv.at[pair], at(p=others[i]))
 
-    for i, p in enumerate(others):
-        sums[p] = residual(p)
+    both = lax.dot_general(wide[...], parts[...], (((1,), (1,)), ((), ())), preferred_element_type=jnp.float32)
+    for p in range(n_pairs):
+        sums[p] = both[p * tall:(p + 1) * tall, 0:2 * n_a] + both[p * tall:(p + 1) * tall, 2 * n_a:4 * n_a]
+    for i in range(len(others)):
         give_sum(i).start()
-    total = residual(pair)
+    total = sums[pair]
     for p in others:
         copy(sums.at[p], inbox.at[p], r_send.at[0], r_recv.at[p], at(p=p)).wait_recv()
         total = total + inbox[p]
@@ -349,10 +342,9 @@
     for i, r in enumerate(sides):
         share(i, r).wait_send()
     pl.when(direct_out)(lambda: cross().wait_send())
-    pl.when(low_edge)(lambda: over(col, False, 0).wait_send())
-    pl.when(low_edge)(lambda: over(col, True, 1).wait_send())
-    pl.when(jnp.logical_and(upper, at_first))(lambda: over(col, True, 1).wait_send())
-    pl.when(high_edge)(lambda: inward().wait_send())
+    pl.when(low_edge)(lambda: over(col, 0).wait_send())
+    pl.when(low_edge)(lambda: over(col, 1).wait_send())
+    pl.when(jnp.logical_and(upper, at_first))(lambda: over(col, 1).wait_send())
     for i in range(len(others)):
         give_weights(i).wait_send()
         give_sum(i).wait_send()
@@ -395,7 +387,7 @@
             dma((n_groups * (GROUP - 1),)), dma((n_cols // 2,)), dma((n_groups + 3,)), dma((n_cols,)),
             dma((n_x - 1,)), dma, dma((n_x,)), dma, dma((n_rows,)),
             dma((n_pairs,)), dma((n_pairs,)), dma((n_pairs,)), dma((n_pairs,)), dma((2,)),
-            pltpu.SemaphoreType.REGULAR,
+            pltpu.SemaphoreType.REGULAR((2,)),
         ],
         compiler_params=pltpu.CompilerParams(
             collective_id=0, has_side_effects=True, vmem_limit_bytes=56 * 1024 * 1024

time: 51.8 us -> 52.3 us (level)
  no operation moved by 1% of the time
where the time goes in v7:
time: 52.3 us; the launch traced here: 51.4 us
  Pallas kernels  49.9 us (95%)
  local copies, waits for them, and re-layouts  1.53 us (3%)
    pallas_call x1, Pallas kernels, body(): pl.pallas_call(functools.partial(kernel, (n_rows, n_cols, n_pairs, slab))...  49.9 us
    unnamed x1, local copies, waits for them, and re-layouts  1.53 us

profile of v7, /device:TPU:1, one launch (start us, length us, event | category | flops | bytes accessed | tf_op | source)
XLA Modules:
  0.0 51.4 jit_solution(6185557098404997627)
XLA Ops:
  0.0 49.9 %ladder.1 = f32[10,16,64]{2,1,0:T(8,128)} custom-call(bf16[2,16,450]{2,1,0:T(8,128)(2,1)} %bitcast.6, bf16[10,16,16]{2,1,0:T(8,128)(2,1)} %amp_hbm.1, s32[512]{0:T(512)} %virt_hbm.1, s32[16]{0:T(128)} %win_hbm.1, s32[120]{0:T(128)} %occ_hbm.1, s32[2,40]{1,0:T(2,128)} %bitcast.7), custom_call_target="tpu_custom_call" | custom-call | tf_op jit(solution)/shard_map/ladder/pallas_call | solution.py:365
  49.9 1.5 %copy.8 = f32[10,64,8,2]{1,3,2,0:T(2,128)} copy(f32[10,64,8,2]{1,3,2,0:T(2,128)} %bitcast.5) | data formatting | bytes 81920

commit v8 on v7

--- a/solution.py
+++ b/solution.py
@@ -201,11 +201,9 @@
 
     expand(pair)
 
-    def onward():
-        for d in range(n_groups - 2, n_groups):
-            g = jnp.where(at_first, group + d, group - d)
-            pl.semaphore_wait(ready.at[d - (n_groups - 2)], 1)
-            over(column(g, place), d - (n_groups - 2)).start()
+    def onward(d, g):
+        pl.semaphore_wait(ready.at[d - (n_groups - 2)], 1)
+        over(column(g, place), d - (n_groups - 2)).start()
 
     def from_right(d):
         g = group + d
@@ -222,6 +220,8 @@
         block(column(g, place), chain_send.at[0], left).wait_recv()
         pl.when(has_right)(lambda: chain(g, right, g).start())
         spread_block(g)
+        if d >= n_groups - 2:
+            pl.when(jnp.logical_and(at_last, lower))(lambda: onward(d, g))
 
     for d in range(1, n_groups):
         pl.when(group + d < n_groups)(functools.partial(from_right, d))
@@ -246,7 +246,8 @@
         for i, r in enumerate(sides):
             share(i, r).start()
 
-    pl.when(low_edge)(onward)
+    for d in range(n_groups - 2, n_groups):
+        pl.when(jnp.logical_and(at_first, lower))(functools.partial(onward, d, group + d))
     pl.when(upper)(from_chain)
     pl.when(direct_in)(from_direct)
     for k in range(n_groups):
@@ -274,35 +275,36 @@
         slot = jnp.bitwise_xor(half, 2 * i)
         copy(b_buf.at[slot], b_buf.at[slot], fan_send.at[0], b_recv.at[slot], at(r=half, c=beside)).wait_recv()
 
+    def b_side(h):
+        return jnp.transpose(jnp.concatenate([b_buf[2 * x + h] for x in range(n_x)], axis=0))
+
+    deep = 2 * GROUP * height
+    a_part = 2 * GROUP * 2
+
+    def contract(k, t, b_rows):
+        g = jnp.bitwise_xor(group, k)
+        rows = a_buf[pl.ds(pl.multiple_of(g * 2 * GROUP, 2 * GROUP), 2 * GROUP)].reshape(deep, LANES)
+        integral[t] = jnp.dot(rows, b_rows, preferred_element_type=jnp.float32)
+        start = pl.multiple_of(t * n_a + g * a_part, a_part)
+        for c in range(width):
+            lines = integral[t, pl.ds(c, a_part, stride=width), :]
+            high = lines.astype(jnp.bfloat16)
+            low = (lines - high.astype(jnp.float32)).astype(jnp.bfloat16)
+            parts[pl.ds(start, a_part), c * span:(c + 1) * span] = high
+            parts[pl.ds(pl.multiple_of(2 * n_a + start, a_part), a_part), c * span:(c + 1) * span] = low
+
+    b_near = b_side(here)
+    for k in range(n_groups):
+        for p in range(GROUP):
+            slot = (jnp.bitwise_xor(group, k) * GROUP + p) * 2 + 1 - core
+            block(slot, mate_send.at[0], mate).wait_recv()
+        contract(k, 0, b_near)
     pl.when(direct_in)(lambda: half_arrived(0))
     for i in range(1, n_x):
         half_arrived(i)
-    b_rows = jnp.concatenate(
-        [b_buf[2 * x + here] for x in range(n_x)] + [b_buf[2 * x + 1 - here] for x in range(n_x)], axis=0
-    )
-    b_rows = jnp.transpose(b_rows)
-    deep = 2 * GROUP * height
-    a_part = 2 * GROUP * 2
-
-    def contract(k):
-        g = jnp.bitwise_xor(group, k)
-        for p in range(GROUP):
-            slot = (g * GROUP + p) * 2 + 1 - core
-            block(slot, mate_send.at[0], mate).wait_recv()
-        rows = a_buf[pl.ds(pl.multiple_of(g * 2 * GROUP, 2 * GROUP), 2 * GROUP)].reshape(deep, LANES)
-        tile = jnp.dot(rows, b_rows, preferred_element_type=jnp.float32)
-        for t in range(2):
-            integral[t] = tile[:, t * span:(t + 1) * span]
-            start = pl.multiple_of(t * n_a + g * a_part, a_part)
-            for c in range(width):
-                lines = integral[t, pl.ds(c, a_part, stride=width), :]
-                high = lines.astype(jnp.bfloat16)
-                low = (lines - high.astype(jnp.float32)).astype(jnp.bfloat16)
-                parts[pl.ds(start, a_part), c * span:(c + 1) * span] = high
-                parts[pl.ds(pl.multiple_of(2 * n_a + start, a_part), a_part), c * span:(c + 1) * span] = low
-
+    b_far = b_side(1 - here)
     for k in range(n_groups):
-        contract(k)
+        contract(k, 1, b_far)
 
     def give_sum(i):
         return copy(sums.at[others[i]], inbox.at[pair], r_send.at[i], r_recv.at[pair], at(p=others[i]))

time: 52.3 us -> 51.3 us (0.981)
  Pallas kernels: 49.9 us -> 48.8 us
    pallas_call x1, Pallas kernels: 49.9 us -> 48.8 us  [body(): pl.pallas_call(functools.partial(kernel, (n_rows, n_cols, n_pairs, slab))...]
where the time goes in v8:
time: 51.3 us; the launch traced here: 50.4 us
  Pallas kernels  48.8 us (95%)
  local copies, waits for them, and re-layouts  1.53 us (3%)
    pallas_call x1, Pallas kernels, body(): pl.pallas_call(functools.partial(kernel, (n_rows, n_cols, n_pairs, slab))...  48.8 us
    unnamed x1, local copies, waits for them, and re-layouts  1.53 us

profile of v8, /device:TPU:1, one launch (start us, length us, event | category | flops | bytes accessed | tf_op | source)
XLA Modules:
  0.0 50.4 jit_solution(12457091149252918137)
XLA Ops:
  0.0 48.8 %ladder.1 = f32[10,16,64]{2,1,0:T(8,128)} custom-call(bf16[2,16,450]{2,1,0:T(8,128)(2,1)} %bitcast.6, bf16[10,16,16]{2,1,0:T(8,128)(2,1)} %amp_hbm.1, s32[512]{0:T(512)} %virt_hbm.1, s32[16]{0:T(128)} %win_hbm.1, s32[120]{0:T(128)} %occ_hbm.1, s32[2,40]{1,0:T(2,128)} %bitcast.7), custom_call_target="tpu_custom_call" | custom-call | tf_op jit(solution)/shard_map/ladder/pallas_call | solution.py:367
  48.8 1.5 %copy.8 = f32[10,64,8,2]{1,3,2,0:T(2,128)} copy(f32[10,64,8,2]{1,3,2,0:T(2,128)} %bitcast.5) | data formatting | bytes 81920

commit v9 on v8

--- a/solution.py
+++ b/solution.py
@@ -38,7 +38,7 @@
         return (row if r is None else r, col if c is None else c, pair if p is None else p)
 
     near = [column(group, jnp.bitwise_xor(place, j)) for j in range(1, GROUP)]
-    beside = near[0]
+    beside = jnp.bitwise_xor(near[0], jnp.where(place < 2, 0, 1))
     mate = jnp.bitwise_xor(col, 1)
     half = jnp.bitwise_xor(row, 1)
     sides = [jnp.bitwise_xor(row, 2 * k) for k in range(1, n_x)]
@@ -64,7 +64,7 @@
         pl.semaphore_signal(barrier, inc=1, device_id=peer, device_id_type=MESH)
 
     peers = [at(c=c) for c in near + [mate]] + [at(r=r) for r in sides] + [at(p=p) for p in others]
-    peers += [at(r=r, c=beside) for r in sides]
+    peers += [at(r=r, c=beside) for r in [row] + sides]
     for peer in peers:
         greet(peer)
     pl.when(has_right)(lambda: greet(at(c=right)))
@@ -173,89 +173,6 @@
         give_weights(i).start()
 
     n_b = n_x * 2
-    span = n_b * width
-    tall = slab * n_b
-    line = lax.broadcasted_iota(jnp.int32, (2 * n_b, span), 0)
-    lane = lax.broadcasted_iota(jnp.int32, (2 * n_b, span), 1)
-    own_b = lax.div(lane, width) == lax.rem(line, n_b)
-    spread = (
-        lax.rem(lax.broadcasted_iota(jnp.int32, (width, span), 1), width)
-        == lax.broadcasted_iota(jnp.int32, (width, span), 0)
-    ).astype(jnp.bfloat16)
-
-    def expand(p):
-        def one(s, carry):
-            lines = jnp.dot(
-                w_buf[p, pl.ds(pl.multiple_of(s * 2 * width, 2 * width), 2 * width), :], spread,
-                preferred_element_type=jnp.float32,
-            )
-            start = pl.multiple_of(p * tall + s * 2 * n_b, 2 * n_b)
-            for c in range(width):
-                first = jnp.broadcast_to(lines[c:c + 1, :], own_b.shape)
-                second = jnp.broadcast_to(lines[width + c:width + c + 1, :], own_b.shape)
-                tile = jnp.where(own_b, jnp.where(line < n_b, first, second), 0.0)
-                wide[pl.ds(start, 2 * n_b), c * span:(c + 1) * span] = tile.astype(jnp.bfloat16)
-            return carry
-
-        lax.fori_loop(0, slab // 2, one, 0)
-
-    expand(pair)
-
-    def onward(d, g):
-        pl.semaphore_wait(ready.at[d - (n_groups - 2)], 1)
-        over(column(g, place), d - (n_groups - 2)).start()
-
-    def from_right(d):
-        g = group + d
-        block(column(g, place), chain_send.at[0], right).wait_recv()
-        if d == 1:
-            pl.when(lower)(lambda: chain(group, right, n_groups + 1).start())
-        pl.when(passes_left)(lambda: chain(g, left, g).start())
-        if d == n_groups - 1:
-            pl.when(jnp.logical_and(upper, at_first))(lambda: over(column(g, place), 1).start())
-        spread_block(g)
-
-    def from_left(d):
-        g = group - d
-        block(column(g, place), chain_send.at[0], left).wait_recv()
-        pl.when(has_right)(lambda: chain(g, right, g).start())
-        spread_block(g)
-        if d >= n_groups - 2:
-            pl.when(jnp.logical_and(at_last, lower))(lambda: onward(d, g))
-
-    for d in range(1, n_groups):
-        pl.when(group + d < n_groups)(functools.partial(from_right, d))
-        pl.when(group - d >= 0)(functools.partial(from_left, d))
-        if d == 1:
-            for p in others:
-                copy(w_buf.at[p], w_buf.at[p], w_send.at[0], w_recv.at[p], at(p=p)).wait_recv()
-                expand(p)
-
-    def handover(k, j):
-        slot = column(jnp.bitwise_xor(group, k), jnp.bitwise_xor(place, j))
-        block(slot, near_send.at[0], near[j - 1]).wait_recv()
-        mate_copy(slot).start()
-
-    def from_direct():
-        cross().wait_recv()
-        for i, r in enumerate([row] + sides):
-            fan(i, r).start()
-
-    def from_chain():
-        share(0, row).wait_recv()
-        for i, r in enumerate(sides):
-            share(i, r).start()
-
-    for d in range(n_groups - 2, n_groups):
-        pl.when(jnp.logical_and(at_first, lower))(functools.partial(onward, d, group + d))
-    pl.when(upper)(from_chain)
-    pl.when(direct_in)(from_direct)
-    for k in range(n_groups):
-        for j in range(1, GROUP):
-            handover(k, j)
-    pl.when(jnp.logical_and(lower, at_last))(from_chain)
-    for r in sides:
-        copy(b_buf.at[r], b_buf.at[r], side_send.at[0], b_recv.at[r], at(r=r)).wait_recv()
     here = jnp.bitwise_and(row, 1)
     n_a = 2 * n_cols
     label_lane = lax.broadcasted_iota(jnp.int32, (n_b, 2 * n_a), 1)
@@ -271,6 +188,89 @@
             there = jnp.where(label_lane < n_a, mine, far)
             label = jnp.bitwise_xor(label, jnp.where(label_line == 2 * x + m, there, 0))
 
+    span = n_b * width
+    tall = slab * n_b
+    line = lax.broadcasted_iota(jnp.int32, (2 * n_b, span), 0)
+    lane = lax.broadcasted_iota(jnp.int32, (2 * n_b, span), 1)
+    own_b = lax.div(lane, width) == lax.rem(line, n_b)
+    spread = (
+        lax.rem(lax.broadcasted_iota(jnp.int32, (width, span), 1), width)
+        == lax.broadcasted_iota(jnp.int32, (width, span), 0)
+    ).astype(jnp.bfloat16)
+
+    def expand(p):
+        def one(s, carry):
+            lines = jnp.dot(
+                w_buf[p, pl.ds(pl.multiple_of(s * 2 * width, 2 * width), 2 * width), :], spread,
+                preferred_element_type=jnp.float32,
+            )
+            start = pl.multiple_of(p * tall + s * 2 * n_b, 2 * n_b)
+            for c in range(width):
+                first = jnp.broadcast_to(lines[c:c + 1, :], own_b.shape)
+                second = jnp.broadcast_to(lines[width + c:width + c + 1, :], own_b.shape)
+                tile = jnp.where(own_b, jnp.where(line < n_b, first, second), 0.0)
+                wide[pl.ds(start, 2 * n_b), c * span:(c + 1) * span] = tile.astype(jnp.bfloat16)
+            return carry
+
+        lax.fori_loop(0, slab // 2, one, 0)
+
+    expand(pair)
+
+    def onward(d, g):
+        pl.semaphore_wait(ready.at[d - (n_groups - 2)], 1)
+        over(column(g, place), d - (n_groups - 2)).start()
+
+    def from_right(d):
+        g = group + d
+        block(column(g, place), chain_send.at[0], right).wait_recv()
+        if d == 1:
+            pl.when(lower)(lambda: chain(group, right, n_groups + 1).start())
+        pl.when(passes_left)(lambda: chain(g, left, g).start())
+        if d == n_groups - 1:
+            pl.when(jnp.logical_and(upper, at_first))(lambda: over(column(g, place), 1).start())
+        spread_block(g)
+
+    def from_left(d):
+        g = group - d
+        block(column(g, place), chain_send.at[0], left).wait_recv()
+        pl.when(has_right)(lambda: chain(g, right, g).start())
+        spread_block(g)
+        if d >= n_groups - 2:
+            pl.when(jnp.logical_and(at_last, lower))(lambda: onward(d, g))
+
+    for d in range(1, n_groups):
+        pl.when(group + d < n_groups)(functools.partial(from_right, d))
+        pl.when(group - d >= 0)(functools.partial(from_left, d))
+        if d == 1:
+            for p in others:
+                copy(w_buf.at[p], w_buf.at[p], w_send.at[0], w_recv.at[p], at(p=p)).wait_recv()
+                expand(p)
+
+    def handover(k, j):
+        slot = column(jnp.bitwise_xor(group, k), jnp.bitwise_xor(place, j))
+        block(slot, near_send.at[0], near[j - 1]).wait_recv()
+        mate_copy(slot).start()
+
+    def from_direct():
+        cross().wait_recv()
+        for i, r in enumerate([row] + sides):
+            fan(i, r).start()
+
+    def from_chain():
+        share(0, row).wait_recv()
+        for i, r in enumerate(sides):
+            share(i, r).start()
+
+    for d in range(n_groups - 2, n_groups):
+        pl.when(jnp.logical_and(at_first, lower))(functools.partial(onward, d, group + d))
+    pl.when(upper)(from_chain)
+    pl.when(direct_in)(from_direct)
+    for k in range(n_groups):
+        for j in range(1, GROUP):
+            handover(k, j)
+    pl.when(jnp.logical_and(lower, at_last))(from_chain)
+    for r in sides:
+        copy(b_buf.at[r], b_buf.at[r], side_send.at[0], b_recv.at[r], at(r=r)).wait_recv()
     def half_arrived(i):
         slot = jnp.bitwise_xor(half, 2 * i)
         copy(b_buf.at[slot], b_buf.at[slot], fan_send.at[0], b_recv.at[slot], at(r=half, c=beside)).wait_recv()

time: 51.3 us -> 51.3 us (level)
  no operation moved by 1% of the time
where the time goes in v9:
time: 51.3 us; the launch traced here: 50.7 us
  Pallas kernels  49.1 us (96%)
  local copies, waits for them, and re-layouts  1.53 us (3%)
    pallas_call x1, Pallas kernels, body(): pl.pallas_call(functools.partial(kernel, (n_rows, n_cols, n_pairs, slab))...  49.1 us
    unnamed x1, local copies, waits for them, and re-layouts  1.53 us

profile of v9, /device:TPU:1, one launch (start us, length us, event | category | flops | bytes accessed | tf_op | source)
XLA Modules:
  0.0 50.7 jit_solution(596923443699301930)
XLA Ops:
  0.0 49.1 %ladder.1 = f32[10,16,64]{2,1,0:T(8,128)} custom-call(bf16[2,16,450]{2,1,0:T(8,128)(2,1)} %bitcast.6, bf16[10,16,16]{2,1,0:T(8,128)(2,1)} %amp_hbm.1, s32[512]{0:T(512)} %virt_hbm.1, s32[16]{0:T(128)} %win_hbm.1, s32[120]{0:T(128)} %occ_hbm.1, s32[2,40]{1,0:T(2,128)} %bitcast.7), custom_call_target="tpu_custom_call" | custom-call | tf_op jit(solution)/shard_map/ladder/pallas_call | solution.py:367
  49.2 1.5 %copy.8 = f32[10,64,8,2]{1,3,2,0:T(2,128)} copy(f32[10,64,8,2]{1,3,2,0:T(2,128)} %bitcast.5) | data formatting | bytes 81920
